TPU v7x, 32 devices: a whole 2x2x4 slice. The times are simulated.
32 devices in a mesh: curve: 8 (over z, x), sub: 4 (over y, core).
Axes of the slice: x: 2, y: 2, z: 4, core: 2. Of those that a mesh axis runs over, the one named last changes fastest.
Arguments:
- load: float32 [3, 32, 64, 128], P(None, 'sub', 'curve'), may hold values from -6 to 6
- plastic: float32 [32, 64, 128], P('sub', 'curve'), may hold values from 0 to 0.95, as said below
- tile_material: int32 [4, 8, 16], P('sub', 'curve'), may hold values from 0 to 4
- moduli: float32 [4], replicated, may hold values from 0.5 to 4
- k_vol: float32 [24, 24], replicated
- k_dev: float32 [24, 24], replicated
Outputs:
- solution: float32 [3, 32, 64, 128], P(None, 'sub', 'curve')
- residual: float32 [3, 32, 64, 128], P(None, 'sub', 'curve')
Inputs may be any that keep to these rules, and one draw needn't show every extreme that they name: `plastic`: zero for voxels that have not yielded, else the share lost.
All inputs are finite; a program needn't handle non-finite values.
Results may differ from a plain program's by a relative error of at most 0.0003.
Values sent between devices are 32-bit elements; how exact they have to be, the bound alone decides.
No kernel may reach another device: no remote copies, remote signals or barrier semaphores. Data moves between devices by JAX's collectives and lax.ppermute only.
A program may use at most 64 MiB of HBM per device.

v0:
```python
import jax
import jax.numpy as jnp
from jax import lax
from jax.sharding import PartitionSpec as P

TILE = 8
MATERIALS = 4
ITERS = 3


ground_spring = 0.5


def shifted(value, axis, by):
    count = lax.axis_size(axis)
    pairs = [(i, i + by) for i in range(count) if 0 <= i + by < count]
    return lax.ppermute(value, axis, pairs)


def padded(block, sides, width):
    for axis, dim in sides:
        count = lax.axis_size(axis)
        forward = [(i, i + 1) for i in range(count - 1)]
        backward = [(target, source) for source, target in forward]
        low = lax.ppermute(
            lax.slice_in_dim(block, block.shape[dim] - width, None, axis=dim), axis, forward
        )
        high = lax.ppermute(lax.slice_in_dim(block, 0, width, axis=dim), axis, backward)
        block = jnp.concatenate([low, block, high], axis=dim)
    return block


def voxel_coefficients(tile_material, moduli, plastic):
    one_hot = (tile_material[..., None] == jnp.arange(1, MATERIALS + 1, dtype=jnp.int32)).astype(
        jnp.float32
    )
    tile_modulus = jnp.sum(one_hot * moduli, axis=-1)
    voxel_modulus = jnp.repeat(jnp.repeat(jnp.repeat(tile_modulus, TILE, 0), TILE, 1), TILE, 2)
    return jnp.stack([voxel_modulus, voxel_modulus * (1.0 - plastic)])


def shift_second(values, along_y):
    if along_y == 0:
        return values
    zeros_col = jnp.zeros(values.shape[:-1] + (1,), values.dtype)
    return jnp.concatenate([zeros_col, values[..., :-1]], axis=-1)


def keep_mask(extended, first_x, first_z):
    size_x = extended.shape[1] - 1
    size_z = extended.shape[2] - 1
    size_y = extended.shape[3]
    occupied = (extended[0] > 0).astype(jnp.float32)
    active = jnp.zeros((size_x, size_z, size_y), jnp.float32)
    for along_x in (0, 1):
        for along_z in (0, 1):
            for along_y in (0, 1):
                contrib = occupied[
                    1 - along_x : 1 - along_x + size_x, 1 - along_z : 1 - along_z + size_z, :
                ]
                active = jnp.maximum(active, shift_second(contrib, along_y))
    index_x = first_x + jnp.arange(size_x, dtype=jnp.int32)
    index_z = first_z + jnp.arange(size_z, dtype=jnp.int32)
    index_y = jnp.arange(size_y, dtype=jnp.int32)
    free = (
        (index_x > 0)[:, None, None] & (index_z > 0)[None, :, None] & (index_y > 0)[None, None, :]
    )
    return active * free.astype(jnp.float32)


def node_forces(bordered, extended, k_vol, k_dev):
    size_x = extended.shape[1] - 1
    size_z = extended.shape[2] - 1
    size_y = extended.shape[3]
    lower = jnp.moveaxis(bordered[:, 0 : size_x + 1], 1, 0)
    upper = jnp.moveaxis(bordered[:, 1 : size_x + 2], 1, 0)
    layer_coef = jnp.moveaxis(extended, 1, 0)
    k_both = jnp.concatenate([k_vol, k_dev], axis=1)

    def assemble(forces, along_x):
        summed = jnp.zeros((3, size_z, size_y), jnp.float32)
        for along_z in (0, 1):
            for along_y in (0, 1):
                contrib = forces[along_x * 4 + along_z * 2 + along_y][
                    :, 1 - along_z : 1 - along_z + size_z, :
                ]
                summed = summed + shift_second(contrib, along_y)
        return summed

    def layer(carried, layer_item):
        lower_nodes, upper_nodes, coef_layer = layer_item
        corners = []
        for source in (lower_nodes, upper_nodes):
            for along_z in (0, 1):
                block = source[:, along_z : along_z + size_z + 1, :]
                corners.append(block)
                zeros_col = jnp.zeros((3, size_z + 1, 1), jnp.float32)
                corners.append(jnp.concatenate([block[:, :, 1:], zeros_col], axis=2))
        element = jnp.concatenate(corners, 0).reshape(24, (size_z + 1) * size_y)
        vol_scale = coef_layer[0].reshape(1, -1)
        dev_scale = coef_layer[1].reshape(1, -1)
        scaled = jnp.concatenate([vol_scale * element, dev_scale * element], axis=0)
        forces = jnp.dot(
            k_both, scaled, precision=lax.Precision.HIGHEST, preferred_element_type=jnp.float32
        )
        forces = forces.reshape(8, 3, size_z + 1, size_y)
        return (assemble(forces, 1), carried + assemble(forces, 0))

    start = jnp.zeros((3, size_z, size_y), jnp.float32)
    _, emitted = lax.scan(layer, start, (lower, upper, layer_coef))
    return jnp.moveaxis(emitted[1:], 0, 1)


def inner_sums(residual, image):
    return lax.psum((jnp.sum(residual * residual), jnp.sum(residual * image)), ("curve", "sub"))


def local(load, plastic, tile_material, moduli, k_vol, k_dev):
    coefficients = voxel_coefficients(tile_material, moduli, plastic)
    below_x = shifted(coefficients[:, -1:], "sub", 1)
    extended = jnp.concatenate([below_x, coefficients], axis=1)
    below_z = shifted(extended[:, :, -1:], "curve", 1)
    extended = jnp.concatenate([below_z, extended], axis=2)
    first_x = lax.axis_index("sub") * coefficients.shape[1]
    first_z = lax.axis_index("curve") * coefficients.shape[2]
    keep = keep_mask(extended, first_x, first_z)

    def operate(field_vals):
        bordered = padded(field_vals, (("curve", 2), ("sub", 1)), 1)
        return keep * (node_forces(bordered, extended, k_vol, k_dev) + ground_spring * field_vals)

    residual = keep * load
    solution = jnp.zeros_like(residual)
    image = operate(residual)
    norm_now, curvature = inner_sums(residual, image)
    step_size = norm_now / curvature
    direction = residual
    carried = image
    for iteration in range(ITERS):
        solution = solution + step_size * direction
        residual = residual - step_size * carried
        if iteration + 1 < ITERS:
            image = operate(residual)
            norm_next, curvature = inner_sums(residual, image)
            next_ratio = norm_next / norm_now
            step_size = norm_next / (curvature - next_ratio * norm_next / step_size)
            direction = residual + next_ratio * direction
            carried = image + next_ratio * carried
            norm_now = norm_next
    return (solution, residual)


def solution(mesh):
    in_specs = (
        P(None, "sub", "curve", None),
        P("sub", "curve", None),
        P("sub", "curve", None),
        P(),
        P(),
        P(),
    )
    out_specs = (P(None, "sub", "curve", None), P(None, "sub", "curve", None))
    return jax.shard_map(local, mesh=mesh, in_specs=in_specs, out_specs=out_specs, check_vma=False)
```

profile of v0, /device:TPU:0, one launch (start us, length us, event | category | flops | bytes accessed | tf_op | source)
XLA Modules:
  0.0 229.4 jit_solution(9882357935380456547)
XLA Ops:
  1.6 0.8 multiply_bitcast_fusion
  2.4 2.4 %collective-permute-start = (f32[2,1,8,128]{3,2,0,1:T(8,128)S(1)}, f32[2,1,8,128]{3,2,0,1:T(8,128)S(1)}, u32[]{:S(2)}, u32[]{:S(2)}) collective-permute-start(f32[2,1,8,128]{3,2,0,1:T(8,128)S(1)} %pad_maximum_fusion.12), channel_id=1, source_target_pairs={{0,1},{1,2},{2,3},{4,5},{5,6},{6,7},{8,9},{9,10},{10,11},{12,13},{... | collective-permute-start | bytes 24584 | tf_op jit(solution)/shard_map/ppermute | solution.py:17
  4.8 0.7 collective-permute-done
  5.6 4.2 %collective-permute-start.1 = (f32[2,9,1,128]{3,2,0,1:T(1,128)S(1)}, f32[2,9,1,128]{3,2,0,1:T(1,128)S(1)}, u32[]{:S(2)}, u32[]{:S(2)}) collective-permute-start(f32[2,9,1,128]{3,2,0,1:T(1,128)S(1)} %pad_maximum_fusion.10), channel_id=1, source_target_pairs={{0,4},{4,8},{8,12},{12,16},{16,20},{20,24},{24,28},{1,5},{5,9},{9,... | collective-permute-start | bytes 27656 | tf_op jit(solution)/shard_map/ppermute | solution.py:17
  9.8 1.3 collective-permute-done.1
  11.4 0.8 copy-done
  12.2 4.2 %collective-permute-start.2 = (f32[3,8,1,128]{3,2,1,0:T(1,128)S(1)}, f32[3,8,1,128]{3,2,1,0:T(1,128)S(1)}, u32[]{:S(2)}, u32[]{:S(2)}) collective-permute-start(f32[3,8,1,128]{3,2,1,0:T(1,128)S(1)} %get-tuple-element.379), channel_id=1, source_target_pairs={{0,4},{4,8},{8,12},{12,16},{16,20},{20,24},{24,28},{1,5},{5,9},{9,... | collective-permute-start | bytes 36872 | tf_op jit(solution)/shard_map/ppermute | solution.py:25
  16.4 1.3 collective-permute-start.3
  17.7 4.6 %collective-permute-done.3 = f32[3,8,1,128]{3,2,1,0:T(1,128)S(1)} collective-permute-done((f32[3,8,1,128]{3,2,1,0:T(1,128)S(1)}, f32[3,8,1,128]{3,2,1,0:T(1,128)S(1)}, u32[]{:S(2)}, u32[]{:S(2)}) %collective-permute-start.3) | collective-permute-done | bytes 12320 | tf_op jit(solution)/shard_map/ppermute | solution.py:28
  22.4 1.4 collective-permute-start.4
  23.8 1.3 collective-permute-start.5
  25.2 5.8 %collective-permute-done.5 = f32[3,1,10,128]{3,2,1,0:T(8,128)S(1)} collective-permute-done((f32[3,1,10,128]{3,2,1,0:T(8,128)S(1)}, f32[3,1,10,128]{3,2,1,0:T(8,128)S(1)}, u32[]{:S(2)}, u32[]{:S(2)}) %collective-permute-start.5) | collective-permute-done | bytes 15392 | tf_op jit(solution)/shard_map/ppermute | solution.py:28
  31.0 9.3 %while.39 = (s32[]{:T(128)}, f32[3,8,128]{2,1,0:T(8,128)S(1)}, f32[9,3,8,128]{3,2,0,1:T(8,128)S(1)}, f32[9,2,9,128]{3,2,1,0:T(8,128)S(1)}, f32[9,3,10,128]{3,2,0...) while((s32[]{:T(128)}, f32[3,8,128]{2,1,0:T(8,128)S(1)}, ...), condition=%wide.region_4.5_spmd.clone, body=%wide.region_3.4_spmd.clone.sunk | while | flops 16060420 | bytes 1924459 | solution.py:110
  40.9 43.1 %all-reduce.30 = (f32[]{:T(128)}, f32[]{:T(128)}) all-reduce(f32[]{:T(128)} %get-tuple-element.256, f32[]{:T(128)} %get-tuple-element.255), channel_id=1, replica_groups=mesh['curve'=8,'sub'=4] {'curve','sub'}, use_global_device_ids=true, to_apply=%region_2.3 | all-reduce | flops 2 | bytes 16 | tf_op jit(solution)/shard_map/psum | solution.py:115
  85.5 4.2 %collective-permute-start.6 = (f32[3,8,1,128]{3,2,1,0:T(1,128)S(1)}, f32[3,8,1,128]{3,2,1,0:T(1,128)S(1)}, u32[]{:S(2)}, u32[]{:S(2)}) collective-permute-start(f32[3,8,1,128]{3,2,1,0:T(1,128)S(1)} %get-tuple-element.377), channel_id=1, source_target_pairs={{0,4},{4,8},{8,12},{12,16},{16,20},{20,24},{24,28},{1,5},{5,9},{9,... | collective-permute-start | bytes 36872 | tf_op jit(solution)/shard_map/ppermute | solution.py:25
  89.6 1.3 collective-permute-start.7
  91.0 4.2 %collective-permute-done.7 = f32[3,8,1,128]{3,2,1,0:T(1,128)S(1)} collective-permute-done((f32[3,8,1,128]{3,2,1,0:T(1,128)S(1)}, f32[3,8,1,128]{3,2,1,0:T(1,128)S(1)}, u32[]{:S(2)}, u32[]{:S(2)}) %collective-permute-start.7) | collective-permute-done | bytes 12320 | tf_op jit(solution)/shard_map/ppermute | solution.py:28
  95.2 1.3 collective-permute-start.8
  96.5 1.3 collective-permute-start.9
  97.9 2.2 collective-permute-done.9
  100.2 9.3 %while.40 = (s32[]{:T(128)}, f32[3,8,128]{2,1,0:T(8,128)S(1)}, f32[9,3,8,128]{3,2,0,1:T(8,128)S(1)}, f32[9,2,9,128]{3,2,1,0:T(8,128)S(1)}, f32[9,3,10,128]{3,2,0...) while((s32[]{:T(128)}, f32[3,8,128]{2,1,0:T(8,128)S(1)}, ...), condition=%wide.region_10.11_spmd.clone, body=%wide.region_9.10_spmd.clone.sunk | while | flops 16060420 | bytes 1924459 | solution.py:110
  109.4 0.7 multiply_reduce_fusion.2
  110.2 42.8 %all-reduce.29 = (f32[]{:T(128)}, f32[]{:T(128)}) all-reduce(f32[]{:T(128)} %get-tuple-element.254, f32[]{:T(128)} %get-tuple-element.253), channel_id=1, replica_groups=mesh['curve'=8,'sub'=4] {'curve','sub'}, use_global_device_ids=true, to_apply=%region_8.9 | all-reduce | flops 2 | bytes 16 | tf_op jit(solution)/shard_map/psum | solution.py:115
  157.4 4.2 %collective-permute-start.10 = (f32[3,8,1,128]{3,2,1,0:T(1,128)S(1)}, f32[3,8,1,128]{3,2,1,0:T(1,128)S(1)}, u32[]{:S(2)}, u32[]{:S(2)}) collective-permute-start(f32[3,8,1,128]{3,2,1,0:T(1,128)S(1)} %get-tuple-element.375), channel_id=1, source_target_pairs={{0,4},{4,8},{8,12},{12,16},{16,20},{20,24},{24,28},{1,5},{5,9},{9,... | collective-permute-start | bytes 36872 | tf_op jit(solution)/shard_map/ppermute | solution.py:25
  161.6 1.3 collective-permute-start.11
  163.0 4.2 %collective-permute-done.11 = f32[3,8,1,128]{3,2,1,0:T(1,128)S(1)} collective-permute-done((f32[3,8,1,128]{3,2,1,0:T(1,128)S(1)}, f32[3,8,1,128]{3,2,1,0:T(1,128)S(1)}, u32[]{:S(2)}, u32[]{:S(2)}) %collective-permute-start.11) | collective-permute-done | bytes 12320 | tf_op jit(solution)/shard_map/ppermute | solution.py:28
  167.2 1.3 collective-permute-start.12
  168.5 1.3 collective-permute-start.13
  169.8 2.3 collective-permute-done.13
  172.2 9.3 %while.41 = (s32[]{:T(128)}, f32[3,8,128]{2,1,0:T(8,128)S(1)}, f32[9,3,8,128]{3,2,0,1:T(8,128)S(1)}, f32[9,2,9,128]{3,2,1,0:T(8,128)S(1)}, f32[9,3,10,128]{3,2,0...) while((s32[]{:T(128)}, f32[3,8,128]{2,1,0:T(8,128)S(1)}, ...), condition=%wide.region_16.17_spmd.clone, body=%wide.region_15.16_spmd.clone.sunk | while | flops 16060420 | bytes 1924459 | solution.py:110
  182.1 42.8 %all-reduce.28 = (f32[]{:T(128)}, f32[]{:T(128)}) all-reduce(f32[]{:T(128)} %get-tuple-element.252, f32[]{:T(128)} %get-tuple-element.251), channel_id=1, replica_groups=mesh['curve'=8,'sub'=4] {'curve','sub'}, use_global_device_ids=true, to_apply=%region_14.15 | all-reduce | flops 2 | bytes 16 | tf_op jit(solution)/shard_map/psum | solution.py:115
  228.7 0.7 multiply_subtract_fusion
  (833 shorter events, 26.3 us)
Async XLA Ops:
  0.6 0.7 copy-start.3
  0.7 0.7 copy-start.4
  2.4 3.2 %collective-permute-start = (f32[2,1,8,128]{3,2,0,1:T(8,128)S(1)}, f32[2,1,8,128]{3,2,0,1:T(8,128)S(1)}, u32[]{:S(2)}, u32[]{:S(2)}) collective-permute-start(f32[2,1,8,128]{3,2,0,1:T(8,128)S(1)} %pad_maximum_fusion.12), channel_id=1, source_target_pairs={{0,1},{1,2},{2,3},{4,5},{5,6},{6,7},{8,9},{9,10},{10,11},{12,13},{... | collective-permute-start | bytes 24584 | tf_op jit(solution)/shard_map/ppermute | solution.py:17
  5.6 5.6 %collective-permute-start.1 = (f32[2,9,1,128]{3,2,0,1:T(1,128)S(1)}, f32[2,9,1,128]{3,2,0,1:T(1,128)S(1)}, u32[]{:S(2)}, u32[]{:S(2)}) collective-permute-start(f32[2,9,1,128]{3,2,0,1:T(1,128)S(1)} %pad_maximum_fusion.10), channel_id=1, source_target_pairs={{0,4},{4,8},{8,12},{12,16},{16,20},{20,24},{24,28},{1,5},{5,9},{9,... | collective-permute-start | bytes 27656 | tf_op jit(solution)/shard_map/ppermute | solution.py:17
  11.2 0.9 copy-start
  12.2 5.6 %collective-permute-start.2 = (f32[3,8,1,128]{3,2,1,0:T(1,128)S(1)}, f32[3,8,1,128]{3,2,1,0:T(1,128)S(1)}, u32[]{:S(2)}, u32[]{:S(2)}) collective-permute-start(f32[3,8,1,128]{3,2,1,0:T(1,128)S(1)} %get-tuple-element.379), channel_id=1, source_target_pairs={{0,4},{4,8},{8,12},{12,16},{16,20},{20,24},{24,28},{1,5},{5,9},{9,... | collective-permute-start | bytes 36872 | tf_op jit(solution)/shard_map/ppermute | solution.py:25
  16.4 6.0 %collective-permute-start.3 = (f32[3,8,1,128]{3,2,1,0:T(1,128)S(1)}, f32[3,8,1,128]{3,2,1,0:T(1,128)S(1)}, u32[]{:S(2)}, u32[]{:S(2)}) collective-permute-start(f32[3,8,1,128]{3,2,1,0:T(1,128)S(1)} %get-tuple-element.380), channel_id=1, source_target_pairs={{4,0},{8,4},{12,8},{16,12},{20,16},{24,20},{28,24},{5,1},{9,5},{13... | collective-permute-start | bytes 36872 | tf_op jit(solution)/shard_map/ppermute | solution.py:28
  22.4 2.7 %copy-start.1 = (f32[24,24]{1,0:T(8,128)S(1)}, f32[24,24]{1,0:T(8,128)}, u32[]{:S(2)}) copy-start(f32[24,24]{1,0:T(8,128)} %param.17) | copy-start | bytes 6916
  22.4 2.7 %copy-start.2 = (f32[24,24]{1,0:T(8,128)S(1)}, f32[24,24]{1,0:T(8,128)}, u32[]{:S(2)}) copy-start(f32[24,24]{1,0:T(8,128)} %param.16) | copy-start | bytes 6916
  22.4 2.8 %collective-permute-start.4 = (f32[3,1,10,128]{3,2,1,0:T(8,128)S(1)}, f32[3,1,10,128]{3,2,1,0:T(8,128)S(1)}, u32[]{:S(2)}, u32[]{:S(2)}) collective-permute-start(f32[3,1,10,128]{3,2,1,0:T(8,128)S(1)} %get-tuple-element.372), channel_id=1, source_target_pairs={{0,1},{1,2},{2,3},{4,5},{5,6},{6,7},{8,9},{9,10},{10,11},{12,13},{... | collective-permute-start | bytes 46088 | tf_op jit(solution)/shard_map/ppermute | solution.py:25
  23.8 7.2 %collective-permute-start.5 = (f32[3,1,10,128]{3,2,1,0:T(8,128)S(1)}, f32[3,1,10,128]{3,2,1,0:T(8,128)S(1)}, u32[]{:S(2)}, u32[]{:S(2)}) collective-permute-start(f32[3,1,10,128]{3,2,1,0:T(8,128)S(1)} %get-tuple-element.371), channel_id=1, source_target_pairs={{1,0},{2,1},{3,2},{5,4},{6,5},{7,6},{9,8},{10,9},{11,10},{13,12},{... | collective-permute-start | bytes 46088 | tf_op jit(solution)/shard_map/ppermute | solution.py:28
  85.5 5.6 %collective-permute-start.6 = (f32[3,8,1,128]{3,2,1,0:T(1,128)S(1)}, f32[3,8,1,128]{3,2,1,0:T(1,128)S(1)}, u32[]{:S(2)}, u32[]{:S(2)}) collective-permute-start(f32[3,8,1,128]{3,2,1,0:T(1,128)S(1)} %get-tuple-element.377), channel_id=1, source_target_pairs={{0,4},{4,8},{8,12},{12,16},{16,20},{20,24},{24,28},{1,5},{5,9},{9,... | collective-permute-start | bytes 36872 | tf_op jit(solution)/shard_map/ppermute | solution.py:25
  89.6 5.6 %collective-permute-start.7 = (f32[3,8,1,128]{3,2,1,0:T(1,128)S(1)}, f32[3,8,1,128]{3,2,1,0:T(1,128)S(1)}, u32[]{:S(2)}, u32[]{:S(2)}) collective-permute-start(f32[3,8,1,128]{3,2,1,0:T(1,128)S(1)} %get-tuple-element.378), channel_id=1, source_target_pairs={{4,0},{8,4},{12,8},{16,12},{20,16},{24,20},{28,24},{5,1},{9,5},{13... | collective-permute-start | bytes 36872 | tf_op jit(solution)/shard_map/ppermute | solution.py:28
  95.2 2.6 %collective-permute-start.8 = (f32[3,1,10,128]{3,2,1,0:T(8,128)S(1)}, f32[3,1,10,128]{3,2,1,0:T(8,128)S(1)}, u32[]{:S(2)}, u32[]{:S(2)}) collective-permute-start(f32[3,1,10,128]{3,2,1,0:T(8,128)S(1)} %get-tuple-element.368), channel_id=1, source_target_pairs={{0,1},{1,2},{2,3},{4,5},{5,6},{6,7},{8,9},{9,10},{10,11},{12,13},{... | collective-permute-start | bytes 46088 | tf_op jit(solution)/shard_map/ppermute | solution.py:25
  96.5 3.5 %collective-permute-start.9 = (f32[3,1,10,128]{3,2,1,0:T(8,128)S(1)}, f32[3,1,10,128]{3,2,1,0:T(8,128)S(1)}, u32[]{:S(2)}, u32[]{:S(2)}) collective-permute-start(f32[3,1,10,128]{3,2,1,0:T(8,128)S(1)} %get-tuple-element.367), channel_id=1, source_target_pairs={{1,0},{2,1},{3,2},{5,4},{6,5},{7,6},{9,8},{10,9},{11,10},{13,12},{... | collective-permute-start | bytes 46088 | tf_op jit(solution)/shard_map/ppermute | solution.py:28
  157.4 5.6 %collective-permute-start.10 = (f32[3,8,1,128]{3,2,1,0:T(1,128)S(1)}, f32[3,8,1,128]{3,2,1,0:T(1,128)S(1)}, u32[]{:S(2)}, u32[]{:S(2)}) collective-permute-start(f32[3,8,1,128]{3,2,1,0:T(1,128)S(1)} %get-tuple-element.375), channel_id=1, source_target_pairs={{0,4},{4,8},{8,12},{12,16},{16,20},{20,24},{24,28},{1,5},{5,9},{9,... | collective-permute-start | bytes 36872 | tf_op jit(solution)/shard_map/ppermute | solution.py:25
  161.6 5.6 %collective-permute-start.11 = (f32[3,8,1,128]{3,2,1,0:T(1,128)S(1)}, f32[3,8,1,128]{3,2,1,0:T(1,128)S(1)}, u32[]{:S(2)}, u32[]{:S(2)}) collective-permute-start(f32[3,8,1,128]{3,2,1,0:T(1,128)S(1)} %get-tuple-element.376), channel_id=1, source_target_pairs={{4,0},{8,4},{12,8},{16,12},{20,16},{24,20},{28,24},{5,1},{9,5},{13... | collective-permute-start | bytes 36872 | tf_op jit(solution)/shard_map/ppermute | solution.py:28
  167.2 2.6 %collective-permute-start.12 = (f32[3,1,10,128]{3,2,1,0:T(8,128)S(1)}, f32[3,1,10,128]{3,2,1,0:T(8,128)S(1)}, u32[]{:S(2)}, u32[]{:S(2)}) collective-permute-start(f32[3,1,10,128]{3,2,1,0:T(8,128)S(1)} %get-tuple-element.364), channel_id=1, source_target_pairs={{0,1},{1,2},{2,3},{4,5},{5,6},{6,7},{8,9},{9,10},{10,11},{12,13},{... | collective-permute-start | bytes 46088 | tf_op jit(solution)/shard_map/ppermute | solution.py:25
  168.5 3.6 %collective-permute-start.13 = (f32[3,1,10,128]{3,2,1,0:T(8,128)S(1)}, f32[3,1,10,128]{3,2,1,0:T(8,128)S(1)}, u32[]{:S(2)}, u32[]{:S(2)}) collective-permute-start(f32[3,1,10,128]{3,2,1,0:T(8,128)S(1)} %get-tuple-element.363), channel_id=1, source_target_pairs={{1,0},{2,1},{3,2},{5,4},{6,5},{7,6},{9,8},{10,9},{11,10},{13,12},{... | collective-permute-start | bytes 46088 | tf_op jit(solution)/shard_map/ppermute | solution.py:28
where the time goes:
time: 231 us; the launch traced here: 229 us
  blocking collectives  129 us (56%)
  starting transfers between devices  30.9 us (13%)
  waiting for transfers between devices  25.7 us (11%)
  local copies, waits for them, and re-layouts  12.1 us (5%)
  between operations  10.5 us (5%)
  other arithmetic  9.69 us (4%)
  matrix products  7.21 us (3%)
  loops' own time  4.67 us (2%)
    psum x3, blocking collectives, inner_sums(): lax.psum((jnp.sum(residual * residual), jnp.sum(residual * image)), ('cur...  129 us
    ppermute x6, waiting for transfers between devices, padded(): lax.ppermute(lax.slice_in_dim(block, 0, width, axis=dim), axis, backward)  23.3 us
    ppermute x6, starting transfers between devices, padded(): lax.ppermute(lax.slice_in_dim(block, block.shape[dim] - width, None, axis...  16.5 us
    ppermute x6, starting transfers between devices, padded(): lax.ppermute(lax.slice_in_dim(block, 0, width, axis=dim), axis, backward)  7.75 us
    dot_general x27, matrix products, layer(): jnp.dot(k_both, scaled, precision=lax.Precision.HIGHEST, preferred_elemen...  7.21 us
    ppermute x2, starting transfers between devices, shifted(): return lax.ppermute(value, axis, pairs)  6.61 us
    another operation x3, loops' own time, node_forces(): _, emitted = lax.scan(layer, start, (lower, upper, layer_coef))  4.67 us
  transfers between devices with their start and end apart: 14, of which 11 were waited for; matrix products, arithmetic and copies ran while one was open for 0% of the time, Pallas kernels for 0%

commit v1 on v0

v1 whole, which is shorter than its diff:
```python
import functools

import jax
import jax.numpy as jnp
from jax import lax
from jax.experimental import pallas as pl
from jax.experimental.pallas import tpu as pltpu
from jax.sharding import PartitionSpec as P

TILE = 8
MATERIALS = 4
ITERS = 3
HALO = ITERS

ground_spring = 0.5

AXES = ("curve", "sub")
PAIRS = ((0, 0), (0, 1), (0, 2), (0, 3), (1, 1), (1, 2), (1, 3), (2, 2), (2, 3))


def round_up(value, to):
    return -(-value // to) * to


def exchange(value, axis, first):
    count = lax.axis_size(axis)
    pairs = []
    for i in range(first, count - 1, 2):
        pairs += [(i, i + 1), (i + 1, i)]
    return lax.ppermute(value, axis, pairs)


def is_odd(axis):
    return lax.axis_index(axis) % 2 == 1


def sub_message_kernel(
    dims, tile_ref, moduli_ref, load_ref, plastic_ref, kv_ref, kd_ref, a_ref, b_ref, modulus_ref, k_ref, scale_ref
):
    nx, nz, ny, tx, tz, ty = dims
    odd = is_odd("sub")
    lane = lax.broadcasted_iota(jnp.int32, (1, ny), 1) // TILE
    for t in range(tx * tz):
        row = jnp.zeros((1, ny), jnp.float32)
        for y in range(ty):
            material = tile_ref[t // tz, t % tz, y]
            value = jnp.float32(0)
            for m in range(MATERIALS):
                value = jnp.where(material == m + 1, moduli_ref[m], value)
            row = jnp.where(lane == y, value, row)
        modulus_ref[t : t + 1, :] = row
    span = HALO * nz

    def put(at, low, high):
        rows = low.shape[0]
        a_ref[at : at + rows, :] = jnp.where(odd, low, high)
        b_ref[at : at + rows, :] = jnp.where(odd, high, low)

    for c in range(3):
        base = c * nx * nz
        put(c * span, load_ref[base : base + span, :], load_ref[base + nx * nz - span : base + nx * nz, :])
    put(3 * span, plastic_ref[0:span, :], plastic_ref[nx * nz - span : nx * nz, :])
    put(4 * span, modulus_ref[0:tz, :], modulus_ref[(tx - 1) * tz : tx * tz, :])

    r32 = lax.broadcasted_iota(jnp.int32, (32, 24), 0)
    m32 = lax.broadcasted_iota(jnp.int32, (32, 24), 1)
    spread_rows = ((m32 == 6 * (r32 // 8) + r32 % 8) & (r32 % 8 < 6)).astype(jnp.bfloat16)
    m24 = lax.broadcasted_iota(jnp.int32, (24, 128), 0)
    n24 = lax.broadcasted_iota(jnp.int32, (24, 128), 1)
    target = (m24 == 6 * (n24 % 64 // 16) + n24 % 8) & (n24 % 8 < 6)
    first_cols = (target & (n24 < 64)).astype(jnp.bfloat16)
    second_cols = (target & (n24 >= 64)).astype(jnp.bfloat16)
    dot = functools.partial(jnp.dot, preferred_element_type=jnp.float32)
    for at, ref in ((0, kv_ref), (32, kd_ref)):
        k = ref[...]
        high = k.astype(jnp.bfloat16)
        low = (k - high.astype(jnp.float32)).astype(jnp.bfloat16)
        part = dot(dot(spread_rows, high).astype(jnp.bfloat16), first_cols)
        part = part + dot(dot(spread_rows, low).astype(jnp.bfloat16), second_cols)
        k_ref[at : at + 32, :] = part.astype(jnp.bfloat16)

    def size(k):
        top = jnp.max(jnp.abs(k), axis=(0, 1), keepdims=True)
        safe = jnp.where(top > 0, top, 1.0)
        return top * jnp.sqrt(jnp.sum((k / safe) ** 2, axis=(0, 1), keepdims=True) * (1.0 / 24))

    mean_modulus = jnp.float32(0)
    for m in range(MATERIALS):
        mean_modulus = mean_modulus + moduli_ref[m] * (1.0 / MATERIALS)
    theta = ground_spring + 6.4 * mean_modulus * (size(kv_ref[...]) + 0.85 * size(kd_ref[...]))
    scale_ref[...] = jnp.broadcast_to(1.0 / theta, (8, 128))


def pick(ref_a, ref_b, odd, low_ref, high_ref):
    a = ref_a[...]
    b = ref_b[...]
    low_ref[...] = jnp.where(odd, a, b)
    high_ref[...] = jnp.where(odd, b, a)


def curve_message_kernel(
    dims, load_ref, plastic_ref, modulus_ref, ra_ref, rb_ref, a_ref, b_ref, low_ref, high_ref
):
    nx, nz, ny, tx, tz, ty = dims
    size_x = nx + 2 * HALO
    pick(ra_ref, rb_ref, is_odd("sub"), low_ref, high_ref)
    odd = is_odd("curve")
    for out_ref, z_first, tile_z in (
        (a_ref, jnp.where(odd, 0, nz - HALO), jnp.where(odd, 0, tz - 1)),
        (b_ref, jnp.where(odd, nz - HALO, 0), jnp.where(odd, tz - 1, 0)),
    ):
        for f in range(4):
            for zl in range(HALO):
                at = (f * HALO + zl) * size_x
                z = z_first + zl
                if f < 3:
                    own = load_ref[pl.ds(f * nx * nz + z, nx, stride=nz), :]
                else:
                    own = plastic_ref[pl.ds(z, nx, stride=nz), :]
                side = f * HALO * nz
                out_ref[at : at + HALO, :] = low_ref[pl.ds(side + z, HALO, stride=nz), :]
                out_ref[at + HALO : at + HALO + nx, :] = own
                out_ref[at + HALO + nx : at + size_x, :] = high_ref[pl.ds(side + z, HALO, stride=nz), :]
        at = 4 * HALO * size_x
        row = low_ref[pl.ds(4 * HALO * nz + tile_z, 1), :]
        out_ref[at : at + HALO, :] = jnp.broadcast_to(row, (HALO, ny))
        for t in range(tx):
            row = modulus_ref[pl.ds(t * tz + tile_z, 1), :]
            first = at + HALO + t * TILE
            out_ref[first : first + TILE, :] = jnp.broadcast_to(row, (TILE, ny))
        row = high_ref[pl.ds(4 * HALO * nz + tile_z, 1), :]
        out_ref[at + HALO + nx : at + size_x, :] = jnp.broadcast_to(row, (HALO, ny))


def product_kernel(
    dims,
    load_ref, plastic_ref, modulus_ref, sa_ref, sb_ref, ca_ref, cb_ref, k_ref, scale_ref,
    w0_ref, w1_ref, w2_ref, w3_ref, gram_ref,
    slow_ref, shigh_ref, clow_ref, chigh_ref, vol_ref, dev_ref, keep_ref, field_ref, split_ref, sum_ref,
):
    nx, nz, ny, tx, tz, ty = dims
    size_x = nx + 2 * HALO
    size_z = nz + 2 * HALO
    pitch = round_up(size_z, 8)
    w_refs = (w0_ref, w1_ref, w2_ref, w3_ref)
    pick(sa_ref, sb_ref, is_odd("sub"), slow_ref, shigh_ref)
    pick(ca_ref, cb_ref, is_odd("curve"), clow_ref, chigh_ref)

    for x in range(size_x - 1):
        if x < HALO:
            source, at, e_row = slow_ref, 3 * HALO * nz + x * nz, 4 * HALO * nz
            e_ref = slow_ref
        elif x < HALO + nx:
            source, at, e_row = plastic_ref, (x - HALO) * nz, (x - HALO) // TILE * tz
            e_ref = modulus_ref
        else:
            source, at, e_row = shigh_ref, 3 * HALO * nz + (x - HALO - nx) * nz, 4 * HALO * nz
            e_ref = shigh_ref
        row = x * pitch + HALO
        dev_ref[row : row + nz, :] = source[at : at + nz, :]
        for t in range(tz):
            value = jnp.broadcast_to(e_ref[e_row + t : e_row + t + 1, :], (TILE, ny))
            vol_ref[row + t * TILE : row + (t + 1) * TILE, :] = value
    for zl in range(HALO):
        for ref, z in ((clow_ref, zl), (chigh_ref, HALO + nz + zl)):
            at = (3 * HALO + zl) * size_x
            dev_ref[pl.ds(z, size_x, stride=pitch), :] = ref[at : at + size_x, :]
            at = 4 * HALO * size_x
            vol_ref[pl.ds(z, size_x, stride=pitch), :] = ref[at : at + size_x, :]
    first_lane = lax.broadcasted_iota(jnp.int32, (8, ny), 1) == 0
    last_lane = lax.broadcasted_iota(jnp.int32, (8, ny), 1) == ny - 1

    x_index = lax.axis_index("sub") * nx - HALO
    x_count = lax.axis_size("sub") * nx
    z_row = lax.broadcasted_iota(jnp.int32, (pitch, ny), 0) + (lax.axis_index("curve") * nz - HALO)
    z_free = (z_row > 0) & (z_row < lax.axis_size("curve") * nz)
    y_free = lax.broadcasted_iota(jnp.int32, (pitch, ny), 1) > 0
    free = (z_free & y_free).astype(jnp.float32)
    row_index = lax.broadcasted_iota(jnp.int32, (pitch, ny), 0)
    for x in range(size_x):
        below = max(x - 1, 0) * pitch
        above = min(x, size_x - 2) * pitch
        e = jnp.maximum(vol_ref[below : below + pitch, :], vol_ref[above : above + pitch, :])
        e = jnp.where(row_index < size_z - 1, e, pltpu.roll(e, 1, 0))
        before = jnp.where(row_index == 0, e, pltpu.roll(e, 1, 0))
        e = jnp.maximum(e, before)
        e = jnp.maximum(e, pltpu.roll(e, 1, 1))
        here = x_index + x
        x_free = jnp.where((here > 0) & (here < x_count), 1.0, 0.0)
        keep_ref[x * pitch : (x + 1) * pitch, :] = jnp.where(e > 0, free * x_free, 0.0)
    for x in range(size_x - 1):
        rows = pl.ds(x * pitch, pitch)
        dev_ref[rows, :] = vol_ref[rows, :] * (1.0 - dev_ref[rows, :])

    def store_node(x, z, value):
        ahead = jnp.where(last_lane, 0.0, pltpu.roll(value, ny - 1, 1))
        both = value + pltpu.roll(ahead, 3, 0)
        field_ref[x, :, z * ny : (z + 1) * ny] = value
        high = both.astype(jnp.bfloat16).astype(jnp.float32)
        split_ref[x, :, z * ny : (z + 1) * ny] = jnp.concatenate([high, both - high], axis=0).astype(jnp.bfloat16)

    blank = jnp.zeros((5, ny), jnp.float32)
    for x in range(size_x):
        for z in range(size_z):
            if z < HALO:
                rows = clow_ref[pl.ds(z * size_x + x, 3, stride=HALO * size_x), :]
            elif z >= HALO + nz:
                rows = chigh_ref[pl.ds((z - HALO - nz) * size_x + x, 3, stride=HALO * size_x), :]
            elif x < HALO:
                rows = slow_ref[pl.ds(x * nz + z - HALO, 3, stride=HALO * nz), :]
            elif x >= HALO + nx:
                rows = shigh_ref[pl.ds((x - HALO - nx) * nz + z - HALO, 3, stride=HALO * nz), :]
            else:
                rows = load_ref[pl.ds((x - HALO) * nz + z - HALO, 3, stride=nx * nz), :]
            value = jnp.concatenate([rows, blank], axis=0) * keep_ref[pl.ds(x * pitch + z, 1), :]
            store_node(x, z, value)

    def save(out_ref):
        for x in range(nx):
            for z in range(nz):
                value = field_ref[x + HALO, 0:3, (z + HALO) * ny : (z + HALO + 1) * ny]
                out_ref[pl.ds(x * nz + z, 3, stride=nx * nz), :] = value

    save(w0_ref)
    kmat = k_ref[...]
    inverse = scale_ref[0:1, 0:1]
    component = (lax.broadcasted_iota(jnp.int32, (8, ny), 0) < 3).astype(jnp.float32) * inverse

    for k in range(1, ITERS + 1):
        sum_ref[...] = jnp.zeros_like(sum_ref)

        def layer(i, _, k=k):
            z = k - 1
            end = size_z - k
            side_low = side_high = None
            while z < end:
                cols = min(2, end - z)
                lanes = cols * ny
                parts = []
                for a in (0, 1):
                    for c in (0, 1):
                        parts.append(split_ref[i + a, :, (z + c) * ny : (z + c) * ny + lanes])
                rhs = jnp.concatenate(parts + parts, axis=0)
                forces = jnp.dot(kmat, rhs, preferred_element_type=jnp.float32)
                for j in range(cols):
                    here = z + j
                    vol = vol_ref[pl.ds(i * pitch + here, 1), :]
                    dev = dev_ref[pl.ds(i * pitch + here, 1), :]
                    g = []
                    for q in range(4):
                        f_vol = forces[8 * q : 8 * q + 8, j * ny : (j + 1) * ny]
                        f_dev = forces[32 + 8 * q : 40 + 8 * q, j * ny : (j + 1) * ny]
                        g.append(vol * f_vol + dev * f_dev)
                    if here >= k:
                        span = slice(here * ny, (here + 1) * ny)
                        total = sum_ref[:, span] + (g[0] + side_low)
                        sum_ref[:, span] = g[2] + side_high
                        behind = jnp.where(first_lane, 0.0, pltpu.roll(total, 1, 1))
                        total = total + pltpu.roll(behind, 5, 0)
                        old = field_ref[i, :, span]
                        keep = keep_ref[pl.ds(i * pitch + here, 1), :]
                        store_node(i, here, old - (component * keep) * (total + ground_spring * old))
                    side_low, side_high = g[1], g[3]
                z += cols
            return 0

        lax.fori_loop(k - 1, size_x - k, layer, 0)
        save(w_refs[k])

    sums = [jnp.zeros((8, ny), jnp.float32) for _ in PAIRS]
    for r in range(3 * nx * nz // 8):
        w = [ref[8 * r : 8 * r + 8, :] for ref in w_refs]
        for n, (i, j) in enumerate(PAIRS):
            sums[n] = sums[n] + w[i] * w[j]
    lane = lax.broadcasted_iota(jnp.int32, (1, ny), 1)
    row = jnp.zeros((1, ny), jnp.float32)
    for n, value in enumerate(sums):
        row = jnp.where(lane == n, jnp.sum(value, axis=(0, 1), keepdims=True), row)
    gram_ref[...] = jnp.broadcast_to(row[None], gram_ref.shape)


def finish_kernel(gram_ref, scale_ref, w0_ref, w1_ref, w2_ref, w3_ref, solution_ref, residual_ref):
    total = jnp.sum(gram_ref[...], axis=0)
    lane = lax.broadcasted_iota(jnp.int32, total.shape, 1)
    gram = {}
    for n, (i, j) in enumerate(PAIRS):
        value = jnp.sum(jnp.where(lane == n, total, 0.0), axis=1, keepdims=True)
        gram[i, j] = gram[j, i] = value

    def inner(p, q):
        result = None
        for i, left in enumerate(p):
            for j, right in enumerate(q):
                if left is not None and right is not None:
                    term = left * right * gram[i, j]
                    result = term if result is None else result + term
        return result

    def axpy(p, scale, q):
        out = []
        for left, right in zip(p, q):
            if right is None:
                out.append(left)
            else:
                out.append(scale * right if left is None else left + scale * right)
        return out

    def image_of(p):
        out = []
        for i in range(ITERS + 1):
            here = p[i]
            before = p[i - 1] if i > 0 else None
            if here is None:
                out.append(None if before is None else -before)
            else:
                out.append(here if before is None else here - before)
        return out

    one = jnp.ones((1, 1), jnp.float32)
    solution = [None] * (ITERS + 1)
    residual = [one] + [None] * ITERS
    image = image_of(residual)
    norm_now = inner(residual, residual)
    step = norm_now / inner(residual, image)
    direction = residual
    carried = image
    for iteration in range(ITERS):
        solution = axpy(solution, step, direction)
        residual = axpy(residual, -step, carried)
        if iteration + 1 < ITERS:
            image = image_of(residual)
            norm_next = inner(residual, residual)
            curvature = inner(residual, image)
            ratio = norm_next / norm_now
            step = norm_next / (curvature - ratio * norm_next / step)
            direction = axpy(residual, ratio, direction)
            carried = axpy(image, ratio, carried)
            norm_now = norm_next
    inverse = scale_ref[0:1, 0:1]
    w_refs = (w0_ref, w1_ref, w2_ref, w3_ref)
    solution = [None if c is None else c * inverse for c in solution]
    for out_ref, coefs in ((solution_ref, solution), (residual_ref, residual)):
        value = None
        for c, ref in zip(coefs, w_refs):
            if c is not None:
                value = c * ref[...] if value is None else value + c * ref[...]
        out_ref[...] = value


def local(load, plastic, tile_material, moduli, k_vol, k_dev):
    nx, nz, ny = plastic.shape
    dims = (nx, nz, ny) + tile_material.shape
    tx, tz = tile_material.shape[:2]
    f32 = jnp.float32
    vmem = pl.BlockSpec(memory_space=pltpu.VMEM)
    smem = pl.BlockSpec(memory_space=pltpu.SMEM)
    shape = jax.ShapeDtypeStruct
    load = load.reshape(3 * nx * nz, ny)
    plastic = plastic.reshape(nx * nz, ny)
    size_x = nx + 2 * HALO
    size_z = nz + 2 * HALO
    pitch = round_up(size_z, 8)
    sub_rows = round_up(4 * HALO * nz + tz, 8)
    curve_rows = round_up((4 * HALO + 1) * size_x, 8)
    count = lax.axis_size("curve") * lax.axis_size("sub")

    sub_a, sub_b, modulus, k_both, scale = pl.pallas_call(
        functools.partial(sub_message_kernel, dims),
        out_shape=(
            shape((sub_rows, ny), f32), shape((sub_rows, ny), f32), shape((round_up(tx * tz, 8), ny), f32),
            shape((64, 128), jnp.bfloat16), shape((8, 128), f32),
        ),
        in_specs=[smem, smem, vmem, vmem, vmem, vmem],
        out_specs=(vmem,) * 5,
        name="sub_message",
    )(tile_material, moduli, load, plastic, k_vol, k_dev)
    sub_a = exchange(sub_a, "sub", 0)
    sub_b = exchange(sub_b, "sub", 1)
    curve_a, curve_b = pl.pallas_call(
        functools.partial(curve_message_kernel, dims),
        out_shape=(shape((curve_rows, ny), f32),) * 2,
        in_specs=[vmem] * 5,
        out_specs=(vmem,) * 2,
        scratch_shapes=[pltpu.VMEM((sub_rows, ny), f32)] * 2,
        name="curve_message",
    )(load, plastic, modulus, sub_a, sub_b)
    curve_a = exchange(curve_a, "curve", 0)
    curve_b = exchange(curve_b, "curve", 1)
    *basis, gram = pl.pallas_call(
        functools.partial(product_kernel, dims),
        out_shape=(shape((3 * nx * nz, ny), f32),) * (ITERS + 1) + (shape((count, 1, ny), f32),),
        in_specs=[vmem] * 9,
        out_specs=(vmem,) * (ITERS + 2),
        scratch_shapes=[
            pltpu.VMEM((sub_rows, ny), f32), pltpu.VMEM((sub_rows, ny), f32),
            pltpu.VMEM((curve_rows, ny), f32), pltpu.VMEM((curve_rows, ny), f32),
            pltpu.VMEM((size_x * pitch, ny), f32), pltpu.VMEM((size_x * pitch, ny), f32),
            pltpu.VMEM((size_x * pitch, ny), f32),
            pltpu.VMEM((size_x, 8, size_z * ny), f32),
            pltpu.VMEM((size_x, 16, size_z * ny), jnp.bfloat16),
            pltpu.VMEM((8, size_z * ny), f32),
        ],
        name="products",
    )(load, plastic, modulus, sub_a, sub_b, curve_a, curve_b, k_both, scale)
    gram = lax.all_to_all(gram, AXES, 0, 0)
    solution_out, residual_out = pl.pallas_call(
        finish_kernel,
        out_shape=(shape((3 * nx * nz, ny), f32),) * 2,
        in_specs=[vmem] * 6,
        out_specs=(vmem,) * 2,
        name="finish",
    )(gram, scale, *basis)
    return solution_out.reshape(3, nx, nz, ny), residual_out.reshape(3, nx, nz, ny)


def solution(mesh):
    in_specs = (
        P(None, "sub", "curve", None),
        P("sub", "curve", None),
        P("sub", "curve", None),
        P(),
        P(),
        P(),
    )
    out_specs = (P(None, "sub", "curve", None), P(None, "sub", "curve", None))
    return jax.shard_map(local, mesh=mesh, in_specs=in_specs, out_specs=out_specs, check_vma=False)
```

time: 231 us -> 50.2 us (0.22)
  blocking collectives: 129 us -> 21.2 us
  starting transfers between devices: 30.9 us -> 4.62 us
  waiting for transfers between devices: 25.7 us -> 2.54 us
  Pallas kernels: 0 us -> 19.6 us
  local copies, waits for them, and re-layouts: 12.1 us -> 1.3 us
  between operations: 10.5 us -> 0.66 us
  other arithmetic: 9.69 us -> 0 us
  matrix products: 7.21 us -> 0 us
  loops' own time: 4.67 us -> 0 us
    psum x3 -> x0, blocking collectives: 129 us -> none  [inner_sums(): lax.psum((jnp.sum(residual * residual), jnp.sum(residual * image)), ('cur...]
    ppermute x14 -> x4, starting transfers between devices: 30.9 us -> 4.62 us  [exchange(): return lax.ppermute(value, axis, pairs)]
    ppermute x14 -> x4, waiting for transfers between devices: 25.7 us -> 2.54 us  [exchange(): return lax.ppermute(value, axis, pairs)]
    all_to_all x0 -> x1, blocking collectives: none -> 21.2 us  [local(): gram = lax.all_to_all(gram, AXES, 0, 0)]
    pallas_call x0 -> x4, Pallas kernels: none -> 19.6 us  [the longest x1 14 us: local(): pl.pallas_call(functools.partial(product_kernel, dims), out_shape=(shape(...]
    dot_general x27 -> x0, matrix products: 7.21 us -> none  [layer(): jnp.dot(k_both, scaled, precision=lax.Precision.HIGHEST, preferred_elemen...]
    slice x193 -> x0, local copies, waits for them, and re-layouts: 5.59 us -> none  [the longest x54 4.33 us: layer(): corners.append(jnp.concatenate([block[:, :, 1:], zeros_col], axis=2))]
    another operation x3 -> x0, loops' own time: 4.67 us -> none  [node_forces(): _, emitted = lax.scan(layer, start, (lower, upper, layer_coef))]
  transfers between devices with their start and end apart: 14 -> 4, of which waited for: 11 -> 2; matrix products, arithmetic and copies ran while one was open for 0% -> 0% of each run, Pallas kernels for 0% -> 0%
where the time goes in v1:
time: 50.2 us; the launch traced here: 49.9 us
  blocking collectives  21.2 us (42%)
  Pallas kernels  19.6 us (39%)
  starting transfers between devices  4.62 us (9%)
  waiting for transfers between devices  2.54 us (5%)
  local copies, waits for them, and re-layouts  1.3 us (3%)
  between operations  0.66 us (1%)
    all_to_all x1, blocking collectives, local(): gram = lax.all_to_all(gram, AXES, 0, 0)  21.2 us
    pallas_call x1, Pallas kernels, local(): pl.pallas_call(functools.partial(product_kernel, dims), out_shape=(shape(...  14 us
    ppermute x4, starting transfers between devices, exchange(): return lax.ppermute(value, axis, pairs)  4.62 us
    ppermute x4, waiting for transfers between devices, exchange(): return lax.ppermute(value, axis, pairs)  2.54 us
    pallas_call x1, Pallas kernels, local(): pl.pallas_call(finish_kernel, out_shape=(shape((3 * nx * nz, ny), f32),)...  1.93 us
    pallas_call x1, Pallas kernels, local(): pl.pallas_call(functools.partial(sub_message_kernel, dims), out_shape=(sh...  1.91 us
    pallas_call x1, Pallas kernels, local(): pl.pallas_call(functools.partial(curve_message_kernel, dims), out_shape=(...  1.67 us
    unnamed x8, local copies, waits for them, and re-layouts  1.3 us
  transfers between devices with their start and end apart: 4, of which 2 were waited for; matrix products, arithmetic and copies ran while one was open for 0% of the time, Pallas kernels for 0%

profile of v1, /device:TPU:0, one launch (start us, length us, event | category | flops | bytes accessed | tf_op | source)
XLA Modules:
  0.0 49.9 jit_solution(3596586228153677714)
XLA Ops:
  0.6 1.9 %sub_message.1 = (f32[104,128]{1,0:T(8,128)}, f32[104,128]{1,0:T(8,128)}, f32[8,128]{1,0:T(8,128)}, bf16[64,128]{1,0:T(8,128)(2,1)}, f32[8,128]{1,0:T(8,128)}) custom-call(s32[1,1,16]{2,1,0:T(1,128)} %tile_ref.1, f32[4]{0:T(128)} %moduli_ref.1, f32[192,128]{1,0:T(8,128)} %bitcast.4, f32[64,128]{1,0:T(8,128)} %bitcast.7, f32[24,24]{1,0:T(8,128)} %kv_ref.1, ...), custom_call_target="tpu_custom_call" | custom-call | tf_op jit(solution)/shard_map/sub_message/pallas_call | solution.py:367
  2.5 0.5 collective-permute-start
  3.0 0.7 %collective-permute-start.1 = (f32[104,128]{1,0:T(8,128)}, f32[104,128]{1,0:T(8,128)S(1)}, u32[]{:S(2)}, u32[]{:S(2)}) collective-permute-start(f32[104,128]{1,0:T(8,128)} %get-tuple-element.18), channel_id=1, source_target_pairs={{1,2},{2,1},{5,6},{6,5},{9,10},{10,9},{13,14},{14,13},{17,18},{18,... | collective-permute-start | bytes 159752 | tf_op jit(solution)/shard_map/ppermute | solution.py:30
  3.7 0.4 collective-permute-done.ra_ref.sa_ref
  4.1 0.0 copy-start
  4.1 0.0 collective-permute-done.1.rb_ref.sb_ref
  4.1 0.0 copy-start.1
  4.1 0.6 %copy-done = f32[104,128]{1,0:T(8,128)} copy-done((f32[104,128]{1,0:T(8,128)}, f32[104,128]{1,0:T(8,128)S(1)}, u32[]{:S(2)}) %copy-start) | copy-done | bytes 53272
  4.7 0.0 copy-done.1
  4.8 1.7 %curve_message.1 = (f32[184,128]{1,0:T(8,128)}, f32[184,128]{1,0:T(8,128)}) custom-call(f32[192,128]{1,0:T(8,128)} %bitcast.5, f32[64,128]{1,0:T(8,128)} %bitcast.8, f32[8,128]{1,0:T(8,128)} %get-tuple-element.16.modulus_ref, f32[104,128]{1,0:T(8,128)} %copy-done, f32[104,128]{1,0:T(8,128)} %copy-done.1), custom_call_target="tpu_custom_call" | custom-call | tf_op jit(solution)/shard_map/curve_message/pallas_call | solution.py:379
  6.4 2.8 %collective-permute-start.2 = (f32[184,128]{1,0:T(8,128)}, f32[184,128]{1,0:T(8,128)S(1)}, u32[]{:S(2)}, u32[]{:S(2)}) collective-permute-start(f32[184,128]{1,0:T(8,128)} %get-tuple-element.19), channel_id=1, source_target_pairs={{0,4},{4,0},{8,12},{12,8},{16,20},{20,16},{24,28},{28,24},{1,5},{5... | collective-permute-start | bytes 282632 | tf_op jit(solution)/shard_map/ppermute | solution.py:30
  9.3 0.7 %collective-permute-start.3 = (f32[184,128]{1,0:T(8,128)}, f32[184,128]{1,0:T(8,128)S(1)}, u32[]{:S(2)}, u32[]{:S(2)}) collective-permute-start(f32[184,128]{1,0:T(8,128)} %get-tuple-element.20), channel_id=1, source_target_pairs={{4,8},{8,4},{12,16},{16,12},{20,24},{24,20},{5,9},{9,5},{13,17},{1... | collective-permute-start | bytes 282632 | tf_op jit(solution)/shard_map/ppermute | solution.py:30
  9.9 2.1 %collective-permute-done.2.ca_ref = f32[184,128]{1,0:T(8,128)S(1)} collective-permute-done((f32[184,128]{1,0:T(8,128)}, f32[184,128]{1,0:T(8,128)S(1)}, u32[]{:S(2)}, u32[]{:S(2)}) %collective-permute-start.2) | collective-permute-done | bytes 94240 | tf_op jit(solution)/shard_map/ppermute | solution.py:30
  12.0 0.0 copy-start.2
  12.0 0.0 collective-permute-done.3.cb_ref
  12.0 0.0 copy-start.3
  12.0 0.6 %copy-done.2 = f32[184,128]{1,0:T(8,128)} copy-done((f32[184,128]{1,0:T(8,128)}, f32[184,128]{1,0:T(8,128)S(1)}, u32[]{:S(2)}) %copy-start.2) | copy-done | bytes 94232
  12.7 0.0 copy-done.3
  12.7 14.0 %products.1 = (f32[192,128]{1,0:T(8,128)}, f32[192,128]{1,0:T(8,128)}, f32[192,128]{1,0:T(8,128)}, f32[192,128]{1,0:T(8,128)}, f32[32,1,128]{2,1,0:T(1,128)}) custom-call(f32[192,128]{1,0:T(8,128)} %bitcast.6, f32[64,128]{1,0:T(8,128)} %bitcast.9, f32[8,128]{1,0:T(8,128)} %get-tuple-element.16.modulus_ref, f32[104,128]{1,0:T(8,128)} %copy-done, ...), custom_call_target="tpu_custom_call" | custom-call | tf_op jit(solution)/shard_map/products/pallas_call | solution.py:389
  26.7 21.2 %all_to_all.5.gram_ref = f32[32,1,128]{2,1,0:T(1,128)} all-to-all(f32[32,1,128]{2,1,0:T(1,128)} %get-tuple-element.23), channel_id=1, replica_groups=mesh['curve'=8,'sub'=4] {'curve','sub'}, dimensions={0} | all-to-all | bytes 32768 | tf_op jit(solution)/shard_map/all_to_all | solution.py:405
  47.9 1.9 %finish.1 = (f32[192,128]{1,0:T(8,128)}, f32[192,128]{1,0:T(8,128)}) custom-call(f32[32,1,128]{2,1,0:T(1,128)} %all_to_all.5.gram_ref, f32[8,128]{1,0:T(8,128)} %get-tuple-element.22.scale_ref, f32[192,128]{1,0:T(8,128)} %get-tuple-element.24.w0_ref, f32[192,128]{1,0:T(8,128)} %get-tuple-element.25.w1_ref, f32[192,128]{1,0:T(8,128)} %get-tuple-element.26.w2_ref, ...), custom_call_target="tpu_custom_call" | custom-call | tf_op jit(solution)/shard_map/finish/pallas_call | solution.py:406
Async XLA Ops:
  2.5 1.6 %collective-permute-start = (f32[104,128]{1,0:T(8,128)}, f32[104,128]{1,0:T(8,128)S(1)}, u32[]{:S(2)}, u32[]{:S(2)}) collective-permute-start(f32[104,128]{1,0:T(8,128)} %get-tuple-element.17), channel_id=1, source_target_pairs={{0,1},{1,0},{2,3},{3,2},{4,5},{5,4},{6,7},{7,6},{8,9},{9,8},{10,11... | collective-permute-start | bytes 159752 | tf_op jit(solution)/shard_map/ppermute | solution.py:30
  3.0 1.1 %collective-permute-start.1 = (f32[104,128]{1,0:T(8,128)}, f32[104,128]{1,0:T(8,128)S(1)}, u32[]{:S(2)}, u32[]{:S(2)}) collective-permute-start(f32[104,128]{1,0:T(8,128)} %get-tuple-element.18), channel_id=1, source_target_pairs={{1,2},{2,1},{5,6},{6,5},{9,10},{10,9},{13,14},{14,13},{17,18},{18,... | collective-permute-start | bytes 159752 | tf_op jit(solution)/shard_map/ppermute | solution.py:30
  4.1 0.6 %copy-start = (f32[104,128]{1,0:T(8,128)}, f32[104,128]{1,0:T(8,128)S(1)}, u32[]{:S(2)}) copy-start(f32[104,128]{1,0:T(8,128)S(1)} %collective-permute-done.ra_ref.sa_ref) | copy-start | bytes 159748
  4.1 0.6 %copy-start.1 = (f32[104,128]{1,0:T(8,128)}, f32[104,128]{1,0:T(8,128)S(1)}, u32[]{:S(2)}) copy-start(f32[104,128]{1,0:T(8,128)S(1)} %collective-permute-done.1.rb_ref.sb_ref) | copy-start | bytes 159748
  6.4 5.6 %collective-permute-start.2 = (f32[184,128]{1,0:T(8,128)}, f32[184,128]{1,0:T(8,128)S(1)}, u32[]{:S(2)}, u32[]{:S(2)}) collective-permute-start(f32[184,128]{1,0:T(8,128)} %get-tuple-element.19), channel_id=1, source_target_pairs={{0,4},{4,0},{8,12},{12,8},{16,20},{20,16},{24,28},{28,24},{1,5},{5... | collective-permute-start | bytes 282632 | tf_op jit(solution)/shard_map/ppermute | solution.py:30
  9.3 2.8 %collective-permute-start.3 = (f32[184,128]{1,0:T(8,128)}, f32[184,128]{1,0:T(8,128)S(1)}, u32[]{:S(2)}, u32[]{:S(2)}) collective-permute-start(f32[184,128]{1,0:T(8,128)} %get-tuple-element.20), channel_id=1, source_target_pairs={{4,8},{8,4},{12,16},{16,12},{20,24},{24,20},{5,9},{9,5},{13,17},{1... | collective-permute-start | bytes 282632 | tf_op jit(solution)/shard_map/ppermute | solution.py:30
  12.0 0.6 %copy-start.2 = (f32[184,128]{1,0:T(8,128)}, f32[184,128]{1,0:T(8,128)S(1)}, u32[]{:S(2)}) copy-start(f32[184,128]{1,0:T(8,128)S(1)} %collective-permute-done.2.ca_ref) | copy-start | bytes 282628
  12.0 0.7 %copy-start.3 = (f32[184,128]{1,0:T(8,128)}, f32[184,128]{1,0:T(8,128)S(1)}, u32[]{:S(2)}) copy-start(f32[184,128]{1,0:T(8,128)S(1)} %collective-permute-done.3.cb_ref) | copy-start | bytes 282628

commit v2 on v1

--- a/solution.py
+++ b/solution.py
@@ -229,7 +229,7 @@
     for k in range(1, ITERS + 1):
         sum_ref[...] = jnp.zeros_like(sum_ref)
 
-        def layer(i, _, k=k):
+        for i in range(k - 1, size_x - k):
             z = k - 1
             end = size_z - k
             side_low = side_high = None
@@ -262,9 +262,6 @@
                         store_node(i, here, old - (component * keep) * (total + ground_spring * old))
                     side_low, side_high = g[1], g[3]
                 z += cols
-            return 0
-
-        lax.fori_loop(k - 1, size_x - k, layer, 0)
         save(w_refs[k])
 
     sums = [jnp.zeros((8, ny), jnp.float32) for _ in PAIRS]

time: 50.2 us -> 41.8 us (0.83)
  Pallas kernels: 19.6 us -> 11.2 us
    pallas_call x1, Pallas kernels: 14 us -> 5.71 us  [local(): pl.pallas_call(functools.partial(product_kernel, dims), out_shape=(shape(...]
where the time goes in v2:
time: 41.8 us; the launch traced here: 41.5 us
  blocking collectives  21.2 us (51%)
  Pallas kernels  11.2 us (27%)
  starting transfers between devices  4.62 us (11%)
  waiting for transfers between devices  2.54 us (6%)
  local copies, waits for them, and re-layouts  1.3 us (3%)
  between operations  0.66 us (2%)
    all_to_all x1, blocking collectives, local(): gram = lax.all_to_all(gram, AXES, 0, 0)  21.2 us
    pallas_call x1, Pallas kernels, local(): pl.pallas_call(functools.partial(product_kernel, dims), out_shape=(shape(...  5.71 us
    ppermute x4, starting transfers between devices, exchange(): return lax.ppermute(value, axis, pairs)  4.62 us
    ppermute x4, waiting for transfers between devices, exchange(): return lax.ppermute(value, axis, pairs)  2.54 us
    pallas_call x1, Pallas kernels, local(): pl.pallas_call(finish_kernel, out_shape=(shape((3 * nx * nz, ny), f32),)...  1.93 us
    pallas_call x1, Pallas kernels, local(): pl.pallas_call(functools.partial(sub_message_kernel, dims), out_shape=(sh...  1.91 us
    pallas_call x1, Pallas kernels, local(): pl.pallas_call(functools.partial(curve_message_kernel, dims), out_shape=(...  1.67 us
    unnamed x8, local copies, waits for them, and re-layouts  1.3 us
  transfers between devices with their start and end apart: 4, of which 2 were waited for; matrix products, arithmetic and copies ran while one was open for 0% of the time, Pallas kernels for 0%

profile of v2, /device:TPU:0, one launch (start us, length us, event | category | flops | bytes accessed | tf_op | source)
XLA Modules:
  0.0 41.5 jit_solution(5930184646212086759)
XLA Ops:
  0.6 1.9 %sub_message.1 = (f32[104,128]{1,0:T(8,128)}, f32[104,128]{1,0:T(8,128)}, f32[8,128]{1,0:T(8,128)}, bf16[64,128]{1,0:T(8,128)(2,1)}, f32[8,128]{1,0:T(8,128)}) custom-call(s32[1,1,16]{2,1,0:T(1,128)} %tile_ref.1, f32[4]{0:T(128)} %moduli_ref.1, f32[192,128]{1,0:T(8,128)} %bitcast.4, f32[64,128]{1,0:T(8,128)} %bitcast.7, f32[24,24]{1,0:T(8,128)} %kv_ref.1, ...), custom_call_target="tpu_custom_call" | custom-call | tf_op jit(solution)/shard_map/sub_message/pallas_call | solution.py:364
  2.5 0.5 %collective-permute-start = (f32[104,128]{1,0:T(8,128)}, f32[104,128]{1,0:T(8,128)S(1)}, u32[]{:S(2)}, u32[]{:S(2)}) collective-permute-start(f32[104,128]{1,0:T(8,128)} %get-tuple-element.17), channel_id=1, source_target_pairs={{0,1},{1,0},{2,3},{3,2},{4,5},{5,4},{6,7},{7,6},{8,9},{9,8},{10,11... | collective-permute-start | bytes 159752 | tf_op jit(solution)/shard_map/ppermute | solution.py:30
  3.0 0.7 %collective-permute-start.1 = (f32[104,128]{1,0:T(8,128)}, f32[104,128]{1,0:T(8,128)S(1)}, u32[]{:S(2)}, u32[]{:S(2)}) collective-permute-start(f32[104,128]{1,0:T(8,128)} %get-tuple-element.18), channel_id=1, source_target_pairs={{1,2},{2,1},{5,6},{6,5},{9,10},{10,9},{13,14},{14,13},{17,18},{18,... | collective-permute-start | bytes 159752 | tf_op jit(solution)/shard_map/ppermute | solution.py:30
  3.7 0.4 %collective-permute-done.ra_ref.sa_ref = f32[104,128]{1,0:T(8,128)S(1)} collective-permute-done((f32[104,128]{1,0:T(8,128)}, f32[104,128]{1,0:T(8,128)S(1)}, u32[]{:S(2)}, u32[]{:S(2)}) %collective-permute-start) | collective-permute-done | bytes 53280 | tf_op jit(solution)/shard_map/ppermute | solution.py:30
  4.1 0.0 copy-start
  4.1 0.0 collective-permute-done.1.rb_ref.sb_ref
  4.1 0.0 copy-start.1
  4.1 0.6 %copy-done = f32[104,128]{1,0:T(8,128)} copy-done((f32[104,128]{1,0:T(8,128)}, f32[104,128]{1,0:T(8,128)S(1)}, u32[]{:S(2)}) %copy-start) | copy-done | bytes 53272
  4.7 0.0 copy-done.1
  4.8 1.7 %curve_message.1 = (f32[184,128]{1,0:T(8,128)}, f32[184,128]{1,0:T(8,128)}) custom-call(f32[192,128]{1,0:T(8,128)} %bitcast.5, f32[64,128]{1,0:T(8,128)} %bitcast.8, f32[8,128]{1,0:T(8,128)} %get-tuple-element.16.modulus_ref, f32[104,128]{1,0:T(8,128)} %copy-done, f32[104,128]{1,0:T(8,128)} %copy-done.1), custom_call_target="tpu_custom_call" | custom-call | tf_op jit(solution)/shard_map/curve_message/pallas_call | solution.py:376
  6.4 2.8 %collective-permute-start.2 = (f32[184,128]{1,0:T(8,128)}, f32[184,128]{1,0:T(8,128)S(1)}, u32[]{:S(2)}, u32[]{:S(2)}) collective-permute-start(f32[184,128]{1,0:T(8,128)} %get-tuple-element.19), channel_id=1, source_target_pairs={{0,4},{4,0},{8,12},{12,8},{16,20},{20,16},{24,28},{28,24},{1,5},{5... | collective-permute-start | bytes 282632 | tf_op jit(solution)/shard_map/ppermute | solution.py:30
  9.3 0.7 %collective-permute-start.3 = (f32[184,128]{1,0:T(8,128)}, f32[184,128]{1,0:T(8,128)S(1)}, u32[]{:S(2)}, u32[]{:S(2)}) collective-permute-start(f32[184,128]{1,0:T(8,128)} %get-tuple-element.20), channel_id=1, source_target_pairs={{4,8},{8,4},{12,16},{16,12},{20,24},{24,20},{5,9},{9,5},{13,17},{1... | collective-permute-start | bytes 282632 | tf_op jit(solution)/shard_map/ppermute | solution.py:30
  9.9 2.1 %collective-permute-done.2.ca_ref = f32[184,128]{1,0:T(8,128)S(1)} collective-permute-done((f32[184,128]{1,0:T(8,128)}, f32[184,128]{1,0:T(8,128)S(1)}, u32[]{:S(2)}, u32[]{:S(2)}) %collective-permute-start.2) | collective-permute-done | bytes 94240 | tf_op jit(solution)/shard_map/ppermute | solution.py:30
  12.0 0.0 copy-start.2
  12.0 0.0 collective-permute-done.3.cb_ref
  12.0 0.0 copy-start.3
  12.0 0.6 %copy-done.2 = f32[184,128]{1,0:T(8,128)} copy-done((f32[184,128]{1,0:T(8,128)}, f32[184,128]{1,0:T(8,128)S(1)}, u32[]{:S(2)}) %copy-start.2) | copy-done | bytes 94232
  12.7 0.0 copy-done.3
  12.7 5.7 %products.1 = (f32[192,128]{1,0:T(8,128)}, f32[192,128]{1,0:T(8,128)}, f32[192,128]{1,0:T(8,128)}, f32[192,128]{1,0:T(8,128)}, f32[32,1,128]{2,1,0:T(1,128)}) custom-call(f32[192,128]{1,0:T(8,128)} %bitcast.6, f32[64,128]{1,0:T(8,128)} %bitcast.9, f32[8,128]{1,0:T(8,128)} %get-tuple-element.16.modulus_ref, f32[104,128]{1,0:T(8,128)} %copy-done, ...), custom_call_target="tpu_custom_call" | custom-call | tf_op jit(solution)/shard_map/products/pallas_call | solution.py:386
  18.4 21.2 %all_to_all.5.gram_ref = f32[32,1,128]{2,1,0:T(1,128)} all-to-all(f32[32,1,128]{2,1,0:T(1,128)} %get-tuple-element.23), channel_id=1, replica_groups=mesh['curve'=8,'sub'=4] {'curve','sub'}, dimensions={0} | all-to-all | bytes 32768 | tf_op jit(solution)/shard_map/all_to_all | solution.py:402
  39.6 1.9 %finish.1 = (f32[192,128]{1,0:T(8,128)}, f32[192,128]{1,0:T(8,128)}) custom-call(f32[32,1,128]{2,1,0:T(1,128)} %all_to_all.5.gram_ref, f32[8,128]{1,0:T(8,128)} %get-tuple-element.22.scale_ref, f32[192,128]{1,0:T(8,128)} %get-tuple-element.24.w0_ref, f32[192,128]{1,0:T(8,128)} %get-tuple-element.25.w1_ref, f32[192,128]{1,0:T(8,128)} %get-tuple-element.26.w2_ref, ...), custom_call_target="tpu_custom_call" | custom-call | tf_op jit(solution)/shard_map/finish/pallas_call | solution.py:403
Async XLA Ops:
  2.5 1.6 %collective-permute-start = (f32[104,128]{1,0:T(8,128)}, f32[104,128]{1,0:T(8,128)S(1)}, u32[]{:S(2)}, u32[]{:S(2)}) collective-permute-start(f32[104,128]{1,0:T(8,128)} %get-tuple-element.17), channel_id=1, source_target_pairs={{0,1},{1,0},{2,3},{3,2},{4,5},{5,4},{6,7},{7,6},{8,9},{9,8},{10,11... | collective-permute-start | bytes 159752 | tf_op jit(solution)/shard_map/ppermute | solution.py:30
  3.0 1.1 %collective-permute-start.1 = (f32[104,128]{1,0:T(8,128)}, f32[104,128]{1,0:T(8,128)S(1)}, u32[]{:S(2)}, u32[]{:S(2)}) collective-permute-start(f32[104,128]{1,0:T(8,128)} %get-tuple-element.18), channel_id=1, source_target_pairs={{1,2},{2,1},{5,6},{6,5},{9,10},{10,9},{13,14},{14,13},{17,18},{18,... | collective-permute-start | bytes 159752 | tf_op jit(solution)/shard_map/ppermute | solution.py:30
  4.1 0.6 %copy-start = (f32[104,128]{1,0:T(8,128)}, f32[104,128]{1,0:T(8,128)S(1)}, u32[]{:S(2)}) copy-start(f32[104,128]{1,0:T(8,128)S(1)} %collective-permute-done.ra_ref.sa_ref) | copy-start | bytes 159748
  4.1 0.6 %copy-start.1 = (f32[104,128]{1,0:T(8,128)}, f32[104,128]{1,0:T(8,128)S(1)}, u32[]{:S(2)}) copy-start(f32[104,128]{1,0:T(8,128)S(1)} %collective-permute-done.1.rb_ref.sb_ref) | copy-start | bytes 159748
  6.4 5.6 %collective-permute-start.2 = (f32[184,128]{1,0:T(8,128)}, f32[184,128]{1,0:T(8,128)S(1)}, u32[]{:S(2)}, u32[]{:S(2)}) collective-permute-start(f32[184,128]{1,0:T(8,128)} %get-tuple-element.19), channel_id=1, source_target_pairs={{0,4},{4,0},{8,12},{12,8},{16,20},{20,16},{24,28},{28,24},{1,5},{5... | collective-permute-start | bytes 282632 | tf_op jit(solution)/shard_map/ppermute | solution.py:30
  9.3 2.8 %collective-permute-start.3 = (f32[184,128]{1,0:T(8,128)}, f32[184,128]{1,0:T(8,128)S(1)}, u32[]{:S(2)}, u32[]{:S(2)}) collective-permute-start(f32[184,128]{1,0:T(8,128)} %get-tuple-element.20), channel_id=1, source_target_pairs={{4,8},{8,4},{12,16},{16,12},{20,24},{24,20},{5,9},{9,5},{13,17},{1... | collective-permute-start | bytes 282632 | tf_op jit(solution)/shard_map/ppermute | solution.py:30
  12.0 0.6 %copy-start.2 = (f32[184,128]{1,0:T(8,128)}, f32[184,128]{1,0:T(8,128)S(1)}, u32[]{:S(2)}) copy-start(f32[184,128]{1,0:T(8,128)S(1)} %collective-permute-done.2.ca_ref) | copy-start | bytes 282628
  12.0 0.7 %copy-start.3 = (f32[184,128]{1,0:T(8,128)}, f32[184,128]{1,0:T(8,128)S(1)}, u32[]{:S(2)}) copy-start(f32[184,128]{1,0:T(8,128)S(1)} %collective-permute-done.3.cb_ref) | copy-start | bytes 282628

commit v3 on v2

--- a/solution.py
+++ b/solution.py
@@ -34,11 +34,9 @@
     return lax.axis_index(axis) % 2 == 1
 
 
-def sub_message_kernel(
-    dims, tile_ref, moduli_ref, load_ref, plastic_ref, kv_ref, kd_ref, a_ref, b_ref, modulus_ref, k_ref, scale_ref
-):
+def curve_message_kernel(dims, tile_ref, moduli_ref, load_ref, plastic_ref, a_ref, b_ref, modulus_ref):
     nx, nz, ny, tx, tz, ty = dims
-    odd = is_odd("sub")
+    odd = is_odd("curve")
     lane = lax.broadcasted_iota(jnp.int32, (1, ny), 1) // TILE
     for t in range(tx * tz):
         row = jnp.zeros((1, ny), jnp.float32)
@@ -49,19 +47,24 @@
                 value = jnp.where(material == m + 1, moduli_ref[m], value)
             row = jnp.where(lane == y, value, row)
         modulus_ref[t : t + 1, :] = row
-    span = HALO * nz
-
-    def put(at, low, high):
-        rows = low.shape[0]
-        a_ref[at : at + rows, :] = jnp.where(odd, low, high)
-        b_ref[at : at + rows, :] = jnp.where(odd, high, low)
-
-    for c in range(3):
-        base = c * nx * nz
-        put(c * span, load_ref[base : base + span, :], load_ref[base + nx * nz - span : base + nx * nz, :])
-    put(3 * span, plastic_ref[0:span, :], plastic_ref[nx * nz - span : nx * nz, :])
-    put(4 * span, modulus_ref[0:tz, :], modulus_ref[(tx - 1) * tz : tx * tz, :])
-
+    for out_ref, z_first, tile_z in (
+        (a_ref, jnp.where(odd, 0, nz - HALO), jnp.where(odd, 0, tz - 1)),
+        (b_ref, jnp.where(odd, nz - HALO, 0), jnp.where(odd, tz - 1, 0)),
+    ):
+        for f in range(4):
+            for zl in range(HALO):
+                z = z_first + zl
+                at = (f * HALO + zl) * nx
+                if f < 3:
+                    out_ref[at : at + nx, :] = load_ref[pl.ds(f * nx * nz + z, nx, stride=nz), :]
+                else:
+                    out_ref[at : at + nx, :] = plastic_ref[pl.ds(z, nx, stride=nz), :]
+        for t in range(tx):
+            at = 4 * HALO * nx + t
+            out_ref[at : at + 1, :] = modulus_ref[pl.ds(t * tz + tile_z, 1), :]
+
+
+def setup_kernel(moduli_ref, kv_ref, kd_ref, _, k_ref, scale_ref):
     r32 = lax.broadcasted_iota(jnp.int32, (32, 24), 0)
     m32 = lax.broadcasted_iota(jnp.int32, (32, 24), 1)
     spread_rows = ((m32 == 6 * (r32 // 8) + r32 % 8) & (r32 % 8 < 6)).astype(jnp.bfloat16)
@@ -98,38 +101,31 @@
     high_ref[...] = jnp.where(odd, b, a)
 
 
-def curve_message_kernel(
-    dims, load_ref, plastic_ref, modulus_ref, ra_ref, rb_ref, a_ref, b_ref, low_ref, high_ref
-):
+def sub_message_kernel(dims, load_ref, plastic_ref, modulus_ref, ra_ref, rb_ref, a_ref, b_ref, low_ref, high_ref):
     nx, nz, ny, tx, tz, ty = dims
-    size_x = nx + 2 * HALO
-    pick(ra_ref, rb_ref, is_odd("sub"), low_ref, high_ref)
-    odd = is_odd("curve")
-    for out_ref, z_first, tile_z in (
-        (a_ref, jnp.where(odd, 0, nz - HALO), jnp.where(odd, 0, tz - 1)),
-        (b_ref, jnp.where(odd, nz - HALO, 0), jnp.where(odd, tz - 1, 0)),
+    size_z = nz + 2 * HALO
+    pick(ra_ref, rb_ref, is_odd("curve"), low_ref, high_ref)
+    odd = is_odd("sub")
+    for out_ref, x_first, tile_x in (
+        (a_ref, jnp.where(odd, 0, nx - HALO), jnp.where(odd, 0, tx - 1)),
+        (b_ref, jnp.where(odd, nx - HALO, 0), jnp.where(odd, tx - 1, 0)),
     ):
         for f in range(4):
-            for zl in range(HALO):
-                at = (f * HALO + zl) * size_x
-                z = z_first + zl
+            for xl in range(HALO):
+                at = (f * HALO + xl) * size_z
+                x = x_first + xl
                 if f < 3:
-                    own = load_ref[pl.ds(f * nx * nz + z, nx, stride=nz), :]
+                    own = load_ref[pl.ds(f * nx * nz + x * nz, nz), :]
                 else:
-                    own = plastic_ref[pl.ds(z, nx, stride=nz), :]
-                side = f * HALO * nz
-                out_ref[at : at + HALO, :] = low_ref[pl.ds(side + z, HALO, stride=nz), :]
-                out_ref[at + HALO : at + HALO + nx, :] = own
-                out_ref[at + HALO + nx : at + size_x, :] = high_ref[pl.ds(side + z, HALO, stride=nz), :]
-        at = 4 * HALO * size_x
-        row = low_ref[pl.ds(4 * HALO * nz + tile_z, 1), :]
-        out_ref[at : at + HALO, :] = jnp.broadcast_to(row, (HALO, ny))
-        for t in range(tx):
-            row = modulus_ref[pl.ds(t * tz + tile_z, 1), :]
-            first = at + HALO + t * TILE
-            out_ref[first : first + TILE, :] = jnp.broadcast_to(row, (TILE, ny))
-        row = high_ref[pl.ds(4 * HALO * nz + tile_z, 1), :]
-        out_ref[at + HALO + nx : at + size_x, :] = jnp.broadcast_to(row, (HALO, ny))
+                    own = plastic_ref[pl.ds(x * nz, nz), :]
+                side = f * HALO * nx
+                out_ref[at : at + HALO, :] = low_ref[pl.ds(side + x, HALO, stride=nx), :]
+                out_ref[at + HALO : at + HALO + nz, :] = own
+                out_ref[at + HALO + nz : at + size_z, :] = high_ref[pl.ds(side + x, HALO, stride=nx), :]
+        at = 4 * HALO * size_z
+        out_ref[at : at + 1, :] = low_ref[pl.ds(4 * HALO * nx + tile_x, 1), :]
+        out_ref[at + 1 : at + 1 + tz, :] = modulus_ref[pl.ds(tile_x * tz, tz), :]
+        out_ref[at + 1 + tz : at + 2 + tz, :] = high_ref[pl.ds(4 * HALO * nx + tile_x, 1), :]
 
 
 def product_kernel(
@@ -147,26 +143,29 @@
     pick(ca_ref, cb_ref, is_odd("curve"), clow_ref, chigh_ref)
 
     for x in range(size_x - 1):
-        if x < HALO:
-            source, at, e_row = slow_ref, 3 * HALO * nz + x * nz, 4 * HALO * nz
-            e_ref = slow_ref
-        elif x < HALO + nx:
-            source, at, e_row = plastic_ref, (x - HALO) * nz, (x - HALO) // TILE * tz
-            e_ref = modulus_ref
+        row = x * pitch
+        if HALO <= x < HALO + nx:
+            own = x - HALO
+            dev_ref[row + HALO : row + HALO + nz, :] = plastic_ref[own * nz : (own + 1) * nz, :]
+            e_ref, e_row = modulus_ref, own // TILE * tz
+            rims = (clow_ref, 4 * HALO * nx + own // TILE), (chigh_ref, 4 * HALO * nx + own // TILE)
         else:
-            source, at, e_row = shigh_ref, 3 * HALO * nz + (x - HALO - nx) * nz, 4 * HALO * nz
-            e_ref = shigh_ref
-        row = x * pitch + HALO
-        dev_ref[row : row + nz, :] = source[at : at + nz, :]
+            side_ref, xl = (slow_ref, x) if x < HALO else (shigh_ref, x - HALO - nx)
+            at = (3 * HALO + xl) * size_z
+            dev_ref[row : row + size_z, :] = side_ref[at : at + size_z, :]
+            at = 4 * HALO * size_z
+            e_ref, e_row = side_ref, at + 1
+            rims = (side_ref, at), (side_ref, at + 1 + tz)
         for t in range(tz):
             value = jnp.broadcast_to(e_ref[e_row + t : e_row + t + 1, :], (TILE, ny))
-            vol_ref[row + t * TILE : row + (t + 1) * TILE, :] = value
+            first = row + HALO + t * TILE
+            vol_ref[first : first + TILE, :] = value
+        for (ref, at), first in zip(rims, (row, row + HALO + nz)):
+            vol_ref[first : first + HALO, :] = jnp.broadcast_to(ref[at : at + 1, :], (HALO, ny))
     for zl in range(HALO):
+        at = (3 * HALO + zl) * nx
         for ref, z in ((clow_ref, zl), (chigh_ref, HALO + nz + zl)):
-            at = (3 * HALO + zl) * size_x
-            dev_ref[pl.ds(z, size_x, stride=pitch), :] = ref[at : at + size_x, :]
-            at = 4 * HALO * size_x
-            vol_ref[pl.ds(z, size_x, stride=pitch), :] = ref[at : at + size_x, :]
+            dev_ref[pl.ds(HALO * pitch + z, nx, stride=pitch), :] = ref[at : at + nx, :]
     first_lane = lax.broadcasted_iota(jnp.int32, (8, ny), 1) == 0
     last_lane = lax.broadcasted_iota(jnp.int32, (8, ny), 1) == ny - 1
 
@@ -202,14 +201,14 @@
     blank = jnp.zeros((5, ny), jnp.float32)
     for x in range(size_x):
         for z in range(size_z):
-            if z < HALO:
-                rows = clow_ref[pl.ds(z * size_x + x, 3, stride=HALO * size_x), :]
+            if x < HALO:
+                rows = slow_ref[pl.ds(x * size_z + z, 3, stride=HALO * size_z), :]
+            elif x >= HALO + nx:
+                rows = shigh_ref[pl.ds((x - HALO - nx) * size_z + z, 3, stride=HALO * size_z), :]
+            elif z < HALO:
+                rows = clow_ref[pl.ds(z * nx + x - HALO, 3, stride=HALO * nx), :]
             elif z >= HALO + nz:
-                rows = chigh_ref[pl.ds((z - HALO - nz) * size_x + x, 3, stride=HALO * size_x), :]
-            elif x < HALO:
-                rows = slow_ref[pl.ds(x * nz + z - HALO, 3, stride=HALO * nz), :]
-            elif x >= HALO + nx:
-                rows = shigh_ref[pl.ds((x - HALO - nx) * nz + z - HALO, 3, stride=HALO * nz), :]
+                rows = chigh_ref[pl.ds((z - HALO - nz) * nx + x - HALO, 3, stride=HALO * nx), :]
             else:
                 rows = load_ref[pl.ds((x - HALO) * nz + z - HALO, 3, stride=nx * nz), :]
             value = jnp.concatenate([rows, blank], axis=0) * keep_ref[pl.ds(x * pitch + z, 1), :]
@@ -352,40 +351,49 @@
     vmem = pl.BlockSpec(memory_space=pltpu.VMEM)
     smem = pl.BlockSpec(memory_space=pltpu.SMEM)
     shape = jax.ShapeDtypeStruct
+    kept = pltpu.VMEM
+
+    def near(*values):
+        return [pltpu.with_memory_space_constraint(v, pltpu.VMEM) for v in values]
+
     load = load.reshape(3 * nx * nz, ny)
     plastic = plastic.reshape(nx * nz, ny)
     size_x = nx + 2 * HALO
     size_z = nz + 2 * HALO
     pitch = round_up(size_z, 8)
-    sub_rows = round_up(4 * HALO * nz + tz, 8)
-    curve_rows = round_up((4 * HALO + 1) * size_x, 8)
+    curve_rows = round_up(4 * HALO * nx + tx, 8)
+    sub_rows = round_up(4 * HALO * size_z + tz + 2, 8)
     count = lax.axis_size("curve") * lax.axis_size("sub")
 
-    sub_a, sub_b, modulus, k_both, scale = pl.pallas_call(
+    curve_a, curve_b, modulus = pl.pallas_call(
+        functools.partial(curve_message_kernel, dims),
+        out_shape=(kept((curve_rows, ny), f32), kept((curve_rows, ny), f32), kept((round_up(tx * tz, 8), ny), f32)),
+        in_specs=[smem, smem, vmem, vmem],
+        out_specs=(vmem,) * 3,
+        name="curve_message",
+    )(tile_material, moduli, load, plastic)
+    k_both, scale = pl.pallas_call(
+        setup_kernel,
+        out_shape=(kept((64, 128), jnp.bfloat16), kept((8, 128), f32)),
+        in_specs=[smem, vmem, vmem, vmem],
+        out_specs=(vmem,) * 2,
+        name="setup",
+    )(moduli, k_vol, k_dev, *near(modulus))
+    curve_a = exchange(curve_a, "curve", 0)
+    curve_b = exchange(curve_b, "curve", 1)
+    sub_a, sub_b = pl.pallas_call(
         functools.partial(sub_message_kernel, dims),
-        out_shape=(
-            shape((sub_rows, ny), f32), shape((sub_rows, ny), f32), shape((round_up(tx * tz, 8), ny), f32),
-            shape((64, 128), jnp.bfloat16), shape((8, 128), f32),
-        ),
-        in_specs=[smem, smem, vmem, vmem, vmem, vmem],
-        out_specs=(vmem,) * 5,
+        out_shape=(kept((sub_rows, ny), f32),) * 2,
+        in_specs=[vmem] * 5,
+        out_specs=(vmem,) * 2,
+        scratch_shapes=[pltpu.VMEM((curve_rows, ny), f32)] * 2,
         name="sub_message",
-    )(tile_material, moduli, load, plastic, k_vol, k_dev)
+    )(*near(load, plastic, modulus, curve_a, curve_b))
     sub_a = exchange(sub_a, "sub", 0)
     sub_b = exchange(sub_b, "sub", 1)
-    curve_a, curve_b = pl.pallas_call(
-        functools.partial(curve_message_kernel, dims),
-        out_shape=(shape((curve_rows, ny), f32),) * 2,
-        in_specs=[vmem] * 5,
-        out_specs=(vmem,) * 2,
-        scratch_shapes=[pltpu.VMEM((sub_rows, ny), f32)] * 2,
-        name="curve_message",
-    )(load, plastic, modulus, sub_a, sub_b)
-    curve_a = exchange(curve_a, "curve", 0)
-    curve_b = exchange(curve_b, "curve", 1)
     *basis, gram = pl.pallas_call(
         functools.partial(product_kernel, dims),
-        out_shape=(shape((3 * nx * nz, ny), f32),) * (ITERS + 1) + (shape((count, 1, ny), f32),),
+        out_shape=(kept((3 * nx * nz, ny), f32),) * (ITERS + 1) + (kept((count, 1, ny), f32),),
         in_specs=[vmem] * 9,
         out_specs=(vmem,) * (ITERS + 2),
         scratch_shapes=[
@@ -398,7 +406,7 @@
             pltpu.VMEM((8, size_z * ny), f32),
         ],
         name="products",
-    )(load, plastic, modulus, sub_a, sub_b, curve_a, curve_b, k_both, scale)
+    )(*near(load, plastic, modulus, sub_a, sub_b, curve_a, curve_b, k_both, scale))
     gram = lax.all_to_all(gram, AXES, 0, 0)
     solution_out, residual_out = pl.pallas_call(
         finish_kernel,
@@ -406,7 +414,7 @@
         in_specs=[vmem] * 6,
         out_specs=(vmem,) * 2,
         name="finish",
-    )(gram, scale, *basis)
+    )(*near(gram, scale, *basis))
     return solution_out.reshape(3, nx, nz, ny), residual_out.reshape(3, nx, nz, ny)
 
 

time: 41.8 us -> 34.7 us (0.83)
  Pallas kernels: 11.2 us -> 7.12 us
  local copies, waits for them, and re-layouts: 1.3 us -> 0.01 us
  waiting for transfers between devices: 2.54 us -> 1.46 us
  blocking collectives: 21.2 us -> 20.7 us
    pallas_call x2 -> x3, Pallas kernels: 7.62 us -> 5.2 us  [the longest x1 4.02 us: local(): pl.pallas_call(functools.partial(product_kernel, dims), out_shape=(kept((...]
    unnamed x8 -> x4, local copies, waits for them, and re-layouts: 1.3 us -> 0.01 us
    ppermute x4, waiting for transfers between devices: 2.54 us -> 1.46 us  [exchange(): return lax.ppermute(value, axis, pairs)]
    pallas_call x1, Pallas kernels: 1.93 us -> 0.88 us  [local(): pl.pallas_call(finish_kernel, out_shape=(shape((3 * nx * nz, ny), f32),)...]
    pallas_call x1, Pallas kernels: 1.67 us -> 1.04 us  [local(): pl.pallas_call(functools.partial(curve_message_kernel, dims), out_shape=(...]
    all_to_all x1, blocking collectives: 21.2 us -> 20.7 us  [local(): gram = lax.all_to_all(gram, AXES, 0, 0)]
  transfers between devices with their start and end apart: 4 -> 4, of which waited for: 2 -> 1; matrix products, arithmetic and copies ran while one was open for 0% -> 0% of each run, Pallas kernels for 0% -> 3%
where the time goes in v3:
time: 34.7 us; the launch traced here: 34.4 us
  blocking collectives  20.7 us (60%)
  Pallas kernels  7.12 us (21%)
  starting transfers between devices  4.42 us (13%)
  waiting for transfers between devices  1.46 us (4%)
  between operations  0.72 us (2%)
    all_to_all x1, blocking collectives, local(): gram = lax.all_to_all(gram, AXES, 0, 0)  20.7 us
    ppermute x4, starting transfers between devices, exchange(): return lax.ppermute(value, axis, pairs)  4.42 us
    pallas_call x1, Pallas kernels, local(): pl.pallas_call(functools.partial(product_kernel, dims), out_shape=(kept((...  4.02 us
    ppermute x4, waiting for transfers between devices, exchange(): return lax.ppermute(value, axis, pairs)  1.46 us
    pallas_call x1, Pallas kernels, local(): pl.pallas_call(setup_kernel, out_shape=(kept((64, 128), jnp.bfloat16), ke...  1.12 us
    pallas_call x1, Pallas kernels, local(): pl.pallas_call(functools.partial(curve_message_kernel, dims), out_shape=(...  1.04 us
    pallas_call x1, Pallas kernels, local(): pl.pallas_call(finish_kernel, out_shape=(shape((3 * nx * nz, ny), f32),)...  0.88 us
  transfers between devices with their start and end apart: 4, of which 1 were waited for; matrix products, arithmetic and copies ran while one was open for 0% of the time, Pallas kernels for 3%

profile of v3, /device:TPU:0, one launch (start us, length us, event | category | flops | bytes accessed | tf_op | source)
XLA Modules:
  0.0 34.4 jit_solution(2649050956847804178)
XLA Ops:
  0.6 0.0 copy-start
  0.6 0.0 copy-start.1
  0.6 1.0 %curve_message.1 = (f32[104,128]{1,0:T(8,128)S(1)}, f32[104,128]{1,0:T(8,128)S(1)}, f32[8,128]{1,0:T(8,128)S(1)}) custom-call(s32[1,1,16]{2,1,0:T(1,128)} %tile_ref.1, f32[4]{0:T(128)} %moduli_ref.3, f32[192,128]{1,0:T(8,128)} %bitcast.4, f32[64,128]{1,0:T(8,128)} %bitcast.7), custom_call_target="tpu_custom_call" | custom-call | tf_op jit(solution)/shard_map/curve_message/pallas_call | solution.py:368
  1.7 3.0 %collective-permute-start = (f32[104,128]{1,0:T(8,128)S(1)}, f32[104,128]{1,0:T(8,128)S(1)}, u32[]{:S(2)}, u32[]{:S(2)}) collective-permute-start(f32[104,128]{1,0:T(8,128)S(1)} %get-tuple-element.17), channel_id=1, source_target_pairs={{0,4},{4,0},{8,12},{12,8},{16,20},{20,16},{24,28},{28,24},{1,5},{5... | collective-permute-start | bytes 159752 | tf_op jit(solution)/shard_map/ppermute | solution.py:30
  4.7 0.7 %collective-permute-start.1 = (f32[104,128]{1,0:T(8,128)S(1)}, f32[104,128]{1,0:T(8,128)S(1)}, u32[]{:S(2)}, u32[]{:S(2)}) collective-permute-start(f32[104,128]{1,0:T(8,128)S(1)} %get-tuple-element.18), channel_id=1, source_target_pairs={{4,8},{8,4},{12,16},{16,12},{20,24},{24,20},{5,9},{9,5},{13,17},{1... | collective-permute-start | bytes 159752 | tf_op jit(solution)/shard_map/ppermute | solution.py:30
  5.4 1.5 %collective-permute-done.ra_ref.ca_ref = f32[104,128]{1,0:T(8,128)S(1)} collective-permute-done((f32[104,128]{1,0:T(8,128)S(1)}, f32[104,128]{1,0:T(8,128)S(1)}, u32[]{:S(2)}, u32[]{:S(2)}) %collective-permute-start) | collective-permute-done | bytes 53280 | tf_op jit(solution)/shard_map/ppermute | solution.py:30
  6.8 0.0 collective-permute-done.1.rb_ref.cb_ref
  6.8 0.0 copy-done
  6.8 0.0 copy-done.1
  6.9 0.1 sub_message.1
  6.9 0.1 collective-permute-start.2
  7.0 0.7 %collective-permute-start.3 = (f32[176,128]{1,0:T(8,128)S(1)}, f32[176,128]{1,0:T(8,128)S(1)}, u32[]{:S(2)}, u32[]{:S(2)}) collective-permute-start(f32[176,128]{1,0:T(8,128)S(1)} %get-tuple-element.20), channel_id=1, source_target_pairs={{1,2},{2,1},{5,6},{6,5},{9,10},{10,9},{13,14},{14,13},{17,18},{18,... | collective-permute-start | bytes 270344 | tf_op jit(solution)/shard_map/ppermute | solution.py:30
  7.7 1.1 %setup.1 = (bf16[64,128]{1,0:T(8,128)(2,1)S(1)}, f32[8,128]{1,0:T(8,128)S(1)}) custom-call(f32[4]{0:T(128)} %moduli_ref.3, f32[24,24]{1,0:T(8,128)} %kv_ref.1, f32[24,24]{1,0:T(8,128)} %kd_ref.1, f32[8,128]{1,0:T(8,128)S(1)} %get-tuple-element.16.modulus_ref._), custom_call_target="tpu_custom_call" | custom-call | tf_op jit(solution)/shard_map/setup/pallas_call | solution.py:375
  8.8 0.0 collective-permute-done.2.sa_ref
  8.8 0.0 collective-permute-done.3.sb_ref
  8.8 4.0 %products.1 = (f32[192,128]{1,0:T(8,128)S(1)}, f32[192,128]{1,0:T(8,128)S(1)}, f32[192,128]{1,0:T(8,128)S(1)}, f32[192,128]{1,0:T(8,128)S(1)}, f32[32,1,128]{2,1,0:T(1,128)S(1)}) custom-call(f32[192,128]{1,0:T(8,128)S(1)} %bitcast.6, f32[64,128]{1,0:T(8,128)S(1)} %bitcast.9, f32[8,128]{1,0:T(8,128)S(1)} %get-tuple-element.16.modulus_ref._, ...), custom_call_target="tpu_custom_call" | custom-call | tf_op jit(solution)/shard_map/products/pallas_call | solution.py:394
  12.9 20.7 %all_to_all.5.gram_ref = f32[32,1,128]{2,1,0:T(1,128)S(1)} all-to-all(f32[32,1,128]{2,1,0:T(1,128)S(1)} %get-tuple-element.23), channel_id=1, replica_groups=mesh['curve'=8,'sub'=4] {'curve','sub'}, dimensions={0} | all-to-all | bytes 32768 | tf_op jit(solution)/shard_map/all_to_all | solution.py:410
  33.6 0.9 %finish.1 = (f32[192,128]{1,0:T(8,128)}, f32[192,128]{1,0:T(8,128)}) custom-call(f32[32,1,128]{2,1,0:T(1,128)S(1)} %all_to_all.5.gram_ref, f32[8,128]{1,0:T(8,128)S(1)} %get-tuple-element.22.scale_ref, f32[192,128]{1,0:T(8,128)S(1)} %get-tuple-element.24.w0_ref, f32[192,128]{1,0:T(8,128)S(1)} %get-tuple-element.25.w1_ref, ...), custom_call_target="tpu_custom_call" | custom-call | tf_op jit(solution)/shard_map/finish/pallas_call | solution.py:411
Async XLA Ops:
  0.6 6.2 %copy-start = (f32[3,8,8,128]{3,2,1,0:T(8,128)S(1)}, f32[3,8,8,128]{3,2,1,0:T(8,128)}, u32[]{:S(2)}) copy-start(f32[3,8,8,128]{3,2,1,0:T(8,128)} %param.6) | copy-start | bytes 294916
  0.6 6.2 %copy-start.1 = (f32[8,8,128]{2,1,0:T(8,128)S(1)}, f32[8,8,128]{2,1,0:T(8,128)}, u32[]{:S(2)}) copy-start(f32[8,8,128]{2,1,0:T(8,128)} %param.7) | copy-start | bytes 98308
  1.7 5.1 %collective-permute-start = (f32[104,128]{1,0:T(8,128)S(1)}, f32[104,128]{1,0:T(8,128)S(1)}, u32[]{:S(2)}, u32[]{:S(2)}) collective-permute-start(f32[104,128]{1,0:T(8,128)S(1)} %get-tuple-element.17), channel_id=1, source_target_pairs={{0,4},{4,0},{8,12},{12,8},{16,20},{20,16},{24,28},{28,24},{1,5},{5... | collective-permute-start | bytes 159752 | tf_op jit(solution)/shard_map/ppermute | solution.py:30
  4.7 2.1 %collective-permute-start.1 = (f32[104,128]{1,0:T(8,128)S(1)}, f32[104,128]{1,0:T(8,128)S(1)}, u32[]{:S(2)}, u32[]{:S(2)}) collective-permute-start(f32[104,128]{1,0:T(8,128)S(1)} %get-tuple-element.18), channel_id=1, source_target_pairs={{4,8},{8,4},{12,16},{16,12},{20,24},{24,20},{5,9},{9,5},{13,17},{1... | collective-permute-start | bytes 159752 | tf_op jit(solution)/shard_map/ppermute | solution.py:30
  6.9 1.9 %collective-permute-start.2 = (f32[176,128]{1,0:T(8,128)S(1)}, f32[176,128]{1,0:T(8,128)S(1)}, u32[]{:S(2)}, u32[]{:S(2)}) collective-permute-start(f32[176,128]{1,0:T(8,128)S(1)} %get-tuple-element.19), channel_id=1, source_target_pairs={{0,1},{1,0},{2,3},{3,2},{4,5},{5,4},{6,7},{7,6},{8,9},{9,8},{10,11... | collective-permute-start | bytes 270344 | tf_op jit(solution)/shard_map/ppermute | solution.py:30
  7.0 1.8 %collective-permute-start.3 = (f32[176,128]{1,0:T(8,128)S(1)}, f32[176,128]{1,0:T(8,128)S(1)}, u32[]{:S(2)}, u32[]{:S(2)}) collective-permute-start(f32[176,128]{1,0:T(8,128)S(1)} %get-tuple-element.20), channel_id=1, source_target_pairs={{1,2},{2,1},{5,6},{6,5},{9,10},{10,9},{13,14},{14,13},{17,18},{18,... | collective-permute-start | bytes 270344 | tf_op jit(solution)/shard_map/ppermute | solution.py:30

commit v4 on v3

--- a/solution.py
+++ b/solution.py
@@ -7,6 +7,7 @@
 from jax.experimental.pallas import tpu as pltpu
 from jax.sharding import PartitionSpec as P
 
+
 TILE = 8
 MATERIALS = 4
 ITERS = 3
@@ -15,7 +16,8 @@
 ground_spring = 0.5
 
 AXES = ("curve", "sub")
-PAIRS = ((0, 0), (0, 1), (0, 2), (0, 3), (1, 1), (1, 2), (1, 3), (2, 2), (2, 3))
+MAX_GROWTH = 40.0
+PAIRS = ((0, 0), (0, 1), (0, 2), (0, 3), (1, 1), (1, 2), (1, 3), (2, 2), (2, 3), (3, 3))
 
 
 def round_up(value, to):
@@ -90,7 +92,7 @@
     mean_modulus = jnp.float32(0)
     for m in range(MATERIALS):
         mean_modulus = mean_modulus + moduli_ref[m] * (1.0 / MATERIALS)
-    theta = ground_spring + 6.4 * mean_modulus * (size(kv_ref[...]) + 0.85 * size(kd_ref[...]))
+    theta = ground_spring + 6.6 * mean_modulus * (size(kv_ref[...]) + size(kd_ref[...]))
     scale_ref[...] = jnp.broadcast_to(1.0 / theta, (8, 128))
 
 
@@ -101,8 +103,8 @@
     high_ref[...] = jnp.where(odd, b, a)
 
 
-def sub_message_kernel(dims, load_ref, plastic_ref, modulus_ref, ra_ref, rb_ref, a_ref, b_ref, low_ref, high_ref):
-    nx, nz, ny, tx, tz, ty = dims
+def sub_message_kernel(dims, load_ref, plastic_ref, modulus_ref, ra_ref, rb_ref, _, a_ref, b_ref, low_ref, high_ref):
+    nx, nz, _, tx, tz, _ = dims
     size_z = nz + 2 * HALO
     pick(ra_ref, rb_ref, is_odd("curve"), low_ref, high_ref)
     odd = is_odd("sub")
@@ -134,7 +136,7 @@
     w0_ref, w1_ref, w2_ref, w3_ref, gram_ref,
     slow_ref, shigh_ref, clow_ref, chigh_ref, vol_ref, dev_ref, keep_ref, field_ref, split_ref, sum_ref,
 ):
-    nx, nz, ny, tx, tz, ty = dims
+    nx, nz, ny, _, tz, _ = dims
     size_x = nx + 2 * HALO
     size_z = nz + 2 * HALO
     pitch = round_up(size_z, 8)
@@ -275,7 +277,7 @@
     gram_ref[...] = jnp.broadcast_to(row[None], gram_ref.shape)
 
 
-def finish_kernel(gram_ref, scale_ref, w0_ref, w1_ref, w2_ref, w3_ref, solution_ref, residual_ref):
+def finish_kernel(gram_ref, scale_ref, w0_ref, w1_ref, w2_ref, w3_ref, solution_ref, residual_ref, better_ref, poor_ref):
     total = jnp.sum(gram_ref[...], axis=0)
     lane = lax.broadcasted_iota(jnp.int32, total.shape, 1)
     gram = {}
@@ -317,7 +319,7 @@
     residual = [one] + [None] * ITERS
     image = image_of(residual)
     norm_now = inner(residual, residual)
-    step = norm_now / inner(residual, image)
+    step = first_step = norm_now / inner(residual, image)
     direction = residual
     carried = image
     for iteration in range(ITERS):
@@ -333,6 +335,7 @@
             carried = axpy(image, ratio, carried)
             norm_now = norm_next
     inverse = scale_ref[0:1, 0:1]
+    better_ref[...] = jnp.broadcast_to(first_step * inverse, better_ref.shape)
     w_refs = (w0_ref, w1_ref, w2_ref, w3_ref)
     solution = [None if c is None else c * inverse for c in solution]
     for out_ref, coefs in ((solution_ref, solution), (residual_ref, residual)):
@@ -341,6 +344,12 @@
             if c is not None:
                 value = c * ref[...] if value is None else value + c * ref[...]
         out_ref[...] = value
+    terms = None
+    for i, c in enumerate(residual):
+        size = jnp.abs(c) * jnp.sqrt(gram[i, i])
+        terms = size if terms is None else terms + size
+    well = terms <= MAX_GROWTH * jnp.sqrt(inner(residual, residual))
+    poor_ref[0, 0] = jnp.where(jnp.max(jnp.where(well, 0.0, 1.0)) > 0, 1, 0)
 
 
 def local(load, plastic, tile_material, moduli, k_vol, k_dev):
@@ -379,43 +388,48 @@
         out_specs=(vmem,) * 2,
         name="setup",
     )(moduli, k_vol, k_dev, *near(modulus))
+    curve_b = exchange(curve_b, "curve", 1)
     curve_a = exchange(curve_a, "curve", 0)
-    curve_b = exchange(curve_b, "curve", 1)
     sub_a, sub_b = pl.pallas_call(
         functools.partial(sub_message_kernel, dims),
         out_shape=(kept((sub_rows, ny), f32),) * 2,
-        in_specs=[vmem] * 5,
+        in_specs=[vmem] * 6,
         out_specs=(vmem,) * 2,
         scratch_shapes=[pltpu.VMEM((curve_rows, ny), f32)] * 2,
         name="sub_message",
-    )(*near(load, plastic, modulus, curve_a, curve_b))
+    )(*near(load, plastic, modulus, curve_a, curve_b, scale))
+    sub_b = exchange(sub_b, "sub", 1)
     sub_a = exchange(sub_a, "sub", 0)
-    sub_b = exchange(sub_b, "sub", 1)
-    *basis, gram = pl.pallas_call(
-        functools.partial(product_kernel, dims),
-        out_shape=(kept((3 * nx * nz, ny), f32),) * (ITERS + 1) + (kept((count, 1, ny), f32),),
-        in_specs=[vmem] * 9,
-        out_specs=(vmem,) * (ITERS + 2),
-        scratch_shapes=[
-            pltpu.VMEM((sub_rows, ny), f32), pltpu.VMEM((sub_rows, ny), f32),
-            pltpu.VMEM((curve_rows, ny), f32), pltpu.VMEM((curve_rows, ny), f32),
-            pltpu.VMEM((size_x * pitch, ny), f32), pltpu.VMEM((size_x * pitch, ny), f32),
-            pltpu.VMEM((size_x * pitch, ny), f32),
-            pltpu.VMEM((size_x, 8, size_z * ny), f32),
-            pltpu.VMEM((size_x, 16, size_z * ny), jnp.bfloat16),
-            pltpu.VMEM((8, size_z * ny), f32),
-        ],
-        name="products",
-    )(*near(load, plastic, modulus, sub_a, sub_b, curve_a, curve_b, k_both, scale))
-    gram = lax.all_to_all(gram, AXES, 0, 0)
-    solution_out, residual_out = pl.pallas_call(
-        finish_kernel,
-        out_shape=(shape((3 * nx * nz, ny), f32),) * 2,
-        in_specs=[vmem] * 6,
-        out_specs=(vmem,) * 2,
-        name="finish",
-    )(*near(gram, scale, *basis))
-    return solution_out.reshape(3, nx, nz, ny), residual_out.reshape(3, nx, nz, ny)
+
+    def solve(scale):
+        *basis, gram = pl.pallas_call(
+            functools.partial(product_kernel, dims),
+            out_shape=(kept((3 * nx * nz, ny), f32),) * (ITERS + 1) + (kept((count, 1, ny), f32),),
+            in_specs=[vmem] * 9,
+            out_specs=(vmem,) * (ITERS + 2),
+            scratch_shapes=[
+                pltpu.VMEM((sub_rows, ny), f32), pltpu.VMEM((sub_rows, ny), f32),
+                pltpu.VMEM((curve_rows, ny), f32), pltpu.VMEM((curve_rows, ny), f32),
+                pltpu.VMEM((size_x * pitch, ny), f32), pltpu.VMEM((size_x * pitch, ny), f32),
+                pltpu.VMEM((size_x * pitch, ny), f32),
+                pltpu.VMEM((size_x, 8, size_z * ny), f32),
+                pltpu.VMEM((size_x, 16, size_z * ny), jnp.bfloat16),
+                pltpu.VMEM((8, size_z * ny), f32),
+            ],
+            name="products",
+        )(*near(load, plastic, modulus, sub_a, sub_b, curve_a, curve_b, k_both, scale))
+        gram = lax.all_to_all(gram, AXES, 0, 0)
+        return pl.pallas_call(
+            finish_kernel,
+            out_shape=(shape((3 * nx * nz, ny), f32),) * 2 + (kept((8, 128), f32), pltpu.SMEM((1, 1), jnp.int32)),
+            in_specs=[vmem] * 6,
+            out_specs=(vmem, vmem, vmem, smem),
+            name="finish",
+        )(*near(gram, scale, *basis))
+
+    *found, better, poor = solve(scale)
+    found = lax.cond(poor[0, 0] > 0, lambda: tuple(solve(better)[:2]), lambda: tuple(found))
+    return tuple(value.reshape(3, nx, nz, ny) for value in found)
 
 
 def solution(mesh):
@@ -428,4 +442,5 @@
         P(),
     )
     out_specs = (P(None, "sub", "curve", None), P(None, "sub", "curve", None))
+
     return jax.shard_map(local, mesh=mesh, in_specs=in_specs, out_specs=out_specs, check_vma=False)

time: 34.7 us -> 34.9 us (level)
  blocking collectives: 20.7 us -> 21.3 us
  waiting for transfers between devices: 1.46 us -> 0.94 us
    all_to_all x1, blocking collectives: 20.7 us -> 21.3 us  [solve(): gram = lax.all_to_all(gram, AXES, 0, 0)]
    ppermute x4, waiting for transfers between devices: 1.46 us -> 0.94 us  [exchange(): return lax.ppermute(value, axis, pairs)]
  transfers between devices with their start and end apart: 4 -> 4, of which waited for: 1 -> 2; matrix products, arithmetic and copies ran while one was open for 0% -> 0% of each run, Pallas kernels for 3% -> 3%
where the time goes in v4:
time: 34.9 us; the launch traced here: 34.6 us
  blocking collectives  21.3 us (61%)
  Pallas kernels  7.27 us (21%)
  starting transfers between devices  4.42 us (13%)
  waiting for transfers between devices  0.94 us (3%)
  between operations  0.7 us (2%)
    all_to_all x1, blocking collectives, solve(): gram = lax.all_to_all(gram, AXES, 0, 0)  21.3 us
    ppermute x4, starting transfers between devices, exchange(): return lax.ppermute(value, axis, pairs)  4.42 us
    pallas_call x1, Pallas kernels, solve(): pl.pallas_call(functools.partial(product_kernel, dims), out_shape=(kept((...  4.13 us
    pallas_call x1, Pallas kernels, local(): pl.pallas_call(setup_kernel, out_shape=(kept((64, 128), jnp.bfloat16), ke...  1.12 us
    pallas_call x1, Pallas kernels, local(): pl.pallas_call(functools.partial(curve_message_kernel, dims), out_shape=(...  1.05 us
    ppermute x4, waiting for transfers between devices, exchange(): return lax.ppermute(value, axis, pairs)  0.94 us
    pallas_call x1, Pallas kernels, solve(): pl.pallas_call(finish_kernel, out_shape=(shape((3 * nx * nz, ny), f32),)...  0.91 us
  transfers between devices with their start and end apart: 4, of which 2 were waited for; matrix products, arithmetic and copies ran while one was open for 0% of the time, Pallas kernels for 3%

profile of v4, /device:TPU:0, one launch (start us, length us, event | category | flops | bytes accessed | tf_op | source)
XLA Modules:
  0.0 34.6 jit_solution(10612844426238190378)
XLA Ops:
  0.6 0.0 copy-start
  0.6 1.1 %curve_message.1 = (f32[104,128]{1,0:T(8,128)S(1)}, f32[104,128]{1,0:T(8,128)S(1)}, f32[8,128]{1,0:T(8,128)S(1)}) custom-call(s32[1,1,16]{2,1,0:T(1,128)} %tile_ref.1, f32[4]{0:T(128)} %moduli_ref.3, f32[192,128]{1,0:T(8,128)} %bitcast.7, f32[64,128]{1,0:T(8,128)} %bitcast.11), custom_call_target="tpu_custom_call" | custom-call | tf_op jit(solution)/shard_map/curve_message/pallas_call | solution.py:377
  1.7 0.0 copy-start.1
  1.7 3.0 %collective-permute-start = (f32[104,128]{1,0:T(8,128)S(1)}, f32[104,128]{1,0:T(8,128)S(1)}, u32[]{:S(2)}, u32[]{:S(2)}) collective-permute-start(f32[104,128]{1,0:T(8,128)S(1)} %get-tuple-element.63), channel_id=1, source_target_pairs={{0,4},{4,0},{8,12},{12,8},{16,20},{20,16},{24,28},{28,24},{1,5},{5... | collective-permute-start | bytes 159752 | tf_op jit(solution)/shard_map/ppermute | solution.py:32
  4.7 0.7 %collective-permute-start.1 = (f32[104,128]{1,0:T(8,128)S(1)}, f32[104,128]{1,0:T(8,128)S(1)}, u32[]{:S(2)}, u32[]{:S(2)}) collective-permute-start(f32[104,128]{1,0:T(8,128)S(1)} %get-tuple-element.64), channel_id=1, source_target_pairs={{4,8},{8,4},{12,16},{16,12},{20,24},{24,20},{5,9},{9,5},{13,17},{1... | collective-permute-start | bytes 159752 | tf_op jit(solution)/shard_map/ppermute | solution.py:32
  5.4 1.1 %setup.1 = (bf16[64,128]{1,0:T(8,128)(2,1)S(1)}, f32[8,128]{1,0:T(8,128)S(1)}) custom-call(f32[4]{0:T(128)} %moduli_ref.3, f32[24,24]{1,0:T(8,128)} %kv_ref.1, f32[24,24]{1,0:T(8,128)} %kd_ref.1, f32[8,128]{1,0:T(8,128)S(1)} %get-tuple-element.62._.modulus_ref), custom_call_target="tpu_custom_call" | custom-call | tf_op jit(solution)/shard_map/setup/pallas_call | solution.py:384
  6.5 0.3 collective-permute-done.ra_ref.ca_ref
  6.9 0.0 collective-permute-done.1.rb_ref.cb_ref
  6.9 0.0 copy-done
  6.9 0.0 copy-done.1
  6.9 0.1 sub_message.1
  6.9 0.1 collective-permute-start.2
  7.0 0.7 %collective-permute-start.3 = (f32[176,128]{1,0:T(8,128)S(1)}, f32[176,128]{1,0:T(8,128)S(1)}, u32[]{:S(2)}, u32[]{:S(2)}) collective-permute-start(f32[176,128]{1,0:T(8,128)S(1)} %get-tuple-element.67), channel_id=1, source_target_pairs={{1,2},{2,1},{5,6},{6,5},{9,10},{10,9},{13,14},{14,13},{17,18},{18,... | collective-permute-start | bytes 270344 | tf_op jit(solution)/shard_map/ppermute | solution.py:32
  7.7 0.6 %collective-permute-done.2.sa_ref = f32[176,128]{1,0:T(8,128)S(1)} collective-permute-done((f32[176,128]{1,0:T(8,128)S(1)}, f32[176,128]{1,0:T(8,128)S(1)}, u32[]{:S(2)}, u32[]{:S(2)}) %collective-permute-start.2) | collective-permute-done | bytes 90144 | tf_op jit(solution)/shard_map/ppermute | solution.py:32
  8.3 0.0 collective-permute-done.3.sb_ref
  8.3 4.1 %products.3 = (f32[192,128]{1,0:T(8,128)S(1)}, f32[192,128]{1,0:T(8,128)S(1)}, f32[192,128]{1,0:T(8,128)S(1)}, f32[192,128]{1,0:T(8,128)S(1)}, f32[32,1,128]{2,1,0:T(1,128)S(1)}) custom-call(f32[192,128]{1,0:T(8,128)S(1)} %bitcast.9, f32[64,128]{1,0:T(8,128)S(1)} %bitcast.13, f32[8,128]{1,0:T(8,128)S(1)} %get-tuple-element.62._.modulus_ref, ...), custom_call_target="tpu_custom_call" | custom-call | tf_op jit(solution)/shard_map/products/pallas_call | solution.py:405
  12.4 21.3 %all_to_all.10.gram_ref = f32[32,1,128]{2,1,0:T(1,128)S(1)} all-to-all(f32[32,1,128]{2,1,0:T(1,128)S(1)} %get-tuple-element.69), channel_id=1, replica_groups=mesh['curve'=8,'sub'=4] {'curve','sub'}, dimensions={0} | all-to-all | bytes 32768 | tf_op jit(solution)/shard_map/all_to_all | solution.py:421
  33.7 0.9 %finish.3 = (f32[192,128]{1,0:T(8,128)}, f32[192,128]{1,0:T(8,128)}, f32[8,128]{1,0:T(8,128)S(1)}, s32[1,1]{1,0:T(1,128)S(4)}) custom-call(f32[32,1,128]{2,1,0:T(1,128)S(1)} %all_to_all.10.gram_ref, f32[8,128]{1,0:T(8,128)S(1)} %get-tuple-element.65._.scale_ref, f32[192,128]{1,0:T(8,128)S(1)} %get-tuple-element.70.w0_ref, ...), custom_call_target="tpu_custom_call" | custom-call | tf_op jit(solution)/shard_map/finish/pallas_call | solution.py:422
  (1 shorter events, 0.0 us)
Async XLA Ops:
  0.6 6.2 %copy-start = (f32[3,8,8,128]{3,2,1,0:T(8,128)S(1)}, f32[3,8,8,128]{3,2,1,0:T(8,128)}, u32[]{:S(2)}) copy-start(f32[3,8,8,128]{3,2,1,0:T(8,128)} %param.8) | copy-start | bytes 294916
  1.7 5.2 %copy-start.1 = (f32[8,8,128]{2,1,0:T(8,128)S(1)}, f32[8,8,128]{2,1,0:T(8,128)}, u32[]{:S(2)}) copy-start(f32[8,8,128]{2,1,0:T(8,128)} %param.9) | copy-start | bytes 98308
  1.7 5.1 %collective-permute-start = (f32[104,128]{1,0:T(8,128)S(1)}, f32[104,128]{1,0:T(8,128)S(1)}, u32[]{:S(2)}, u32[]{:S(2)}) collective-permute-start(f32[104,128]{1,0:T(8,128)S(1)} %get-tuple-element.63), channel_id=1, source_target_pairs={{0,4},{4,0},{8,12},{12,8},{16,20},{20,16},{24,28},{28,24},{1,5},{5... | collective-permute-start | bytes 159752 | tf_op jit(solution)/shard_map/ppermute | solution.py:32
  4.7 2.1 %collective-permute-start.1 = (f32[104,128]{1,0:T(8,128)S(1)}, f32[104,128]{1,0:T(8,128)S(1)}, u32[]{:S(2)}, u32[]{:S(2)}) collective-permute-start(f32[104,128]{1,0:T(8,128)S(1)} %get-tuple-element.64), channel_id=1, source_target_pairs={{4,8},{8,4},{12,16},{16,12},{20,24},{24,20},{5,9},{9,5},{13,17},{1... | collective-permute-start | bytes 159752 | tf_op jit(solution)/shard_map/ppermute | solution.py:32
  6.9 1.4 %collective-permute-start.2 = (f32[176,128]{1,0:T(8,128)S(1)}, f32[176,128]{1,0:T(8,128)S(1)}, u32[]{:S(2)}, u32[]{:S(2)}) collective-permute-start(f32[176,128]{1,0:T(8,128)S(1)} %get-tuple-element.66), channel_id=1, source_target_pairs={{0,1},{1,0},{2,3},{3,2},{4,5},{5,4},{6,7},{7,6},{8,9},{9,8},{10,11... | collective-permute-start | bytes 270344 | tf_op jit(solution)/shard_map/ppermute | solution.py:32
  7.0 1.3 %collective-permute-start.3 = (f32[176,128]{1,0:T(8,128)S(1)}, f32[176,128]{1,0:T(8,128)S(1)}, u32[]{:S(2)}, u32[]{:S(2)}) collective-permute-start(f32[176,128]{1,0:T(8,128)S(1)} %get-tuple-element.67), channel_id=1, source_target_pairs={{1,2},{2,1},{5,6},{6,5},{9,10},{10,9},{13,14},{14,13},{17,18},{18,... | collective-permute-start | bytes 270344 | tf_op jit(solution)/shard_map/ppermute | solution.py:32

commit v5 on v4

--- a/solution.py
+++ b/solution.py
@@ -1,3 +1,4 @@
+import collections
 import functools
 
 import jax
@@ -130,78 +131,234 @@
         out_ref[at + 1 + tz : at + 2 + tz, :] = high_ref[pl.ds(4 * HALO * nx + tile_x, 1), :]
 
 
-def product_kernel(
+def inner_rows(nx, level):
+    return range(1, nx) if level == 0 else range(level + 1, nx - level)
+
+
+class Products:
+
+    def __init__(self, dims, kmat, scale_ref):
+        self.nx, self.nz, self.ny = dims[:3]
+        self.size_x = self.nx + 2 * HALO
+        self.size_z = self.nz + 2 * HALO
+        self.pitch = round_up(self.size_z, 8)
+        self.kmat = kmat
+        lane = lax.broadcasted_iota(jnp.int32, (8, self.ny), 1)
+        self.first_lane = lane == 0
+        self.last_lane = lane == self.ny - 1
+        rows = lax.broadcasted_iota(jnp.int32, (8, self.ny), 0)
+        self.component = (rows < 3).astype(jnp.float32) * scale_ref[0:1, 0:1]
+        self.blank = jnp.zeros((5, self.ny), jnp.float32)
+
+    def span(self, z):
+        return slice(z * self.ny, (z + 1) * self.ny)
+
+    def deviatoric(self, refs, x):
+        rows = slice(x * self.pitch, (x + 1) * self.pitch)
+        refs.dev[rows, :] = refs.vol[rows, :] * (1.0 - refs.dev[rows, :])
+
+    def mark_kept(self, refs, layers, vol_at):
+        pitch, shape = self.pitch, (self.pitch, self.ny)
+        x_index = lax.axis_index("sub") * self.nx - HALO
+        x_count = lax.axis_size("sub") * self.nx
+        z_row = lax.broadcasted_iota(jnp.int32, shape, 0)
+        z_index = z_row + (lax.axis_index("curve") * self.nz - HALO)
+        y_free = lax.broadcasted_iota(jnp.int32, shape, 1) > 0
+        free = (z_index > 0) & (z_index < lax.axis_size("curve") * self.nz) & y_free
+        free = free.astype(jnp.float32)
+        for x in layers:
+            below = max(x - 1, 0)
+            above = min(x, self.size_x - 2)
+            e = jnp.maximum(
+                vol_at(below)[below * pitch : (below + 1) * pitch, :],
+                vol_at(above)[above * pitch : (above + 1) * pitch, :],
+            )
+            e = jnp.where(z_row < self.size_z - 1, e, pltpu.roll(e, 1, 0))
+            e = jnp.maximum(e, jnp.where(z_row == 0, e, pltpu.roll(e, 1, 0)))
+            e = jnp.maximum(e, pltpu.roll(e, 1, 1))
+            here = x_index + x
+            x_free = jnp.where((here > 0) & (here < x_count), 1.0, 0.0)
+            refs.keep[x * pitch : (x + 1) * pitch, :] = jnp.where(e > 0, free * x_free, 0.0)
+
+    def store_node(self, refs, x, z, value, w_ref):
+        ny, span = self.ny, self.span(z)
+        ahead = jnp.where(self.last_lane, 0.0, pltpu.roll(value, ny - 1, 1))
+        both = value + pltpu.roll(ahead, 3, 0)
+        refs.field[x, :, span] = value
+        high = both.astype(jnp.bfloat16).astype(jnp.float32)
+        refs.split[x, :, span] = jnp.concatenate([high, both - high], axis=0).astype(jnp.bfloat16)
+        own_x, own_z = x - HALO, z - HALO
+        if 0 <= own_x < self.nx and 0 <= own_z < self.nz:
+            w_ref[pl.ds(own_x * self.nz + own_z, 3, stride=self.nx * self.nz), :] = value[0:3, :]
+
+    def start_node(self, refs, x, z, rows, w_ref):
+        keep = refs.keep[pl.ds(x * self.pitch + z, 1), :]
+        self.store_node(refs, x, z, jnp.concatenate([rows, self.blank], axis=0) * keep, w_ref)
+
+    def update_node(self, refs, held, x, z, total, w_ref):
+        behind = jnp.where(self.first_lane, 0.0, pltpu.roll(total, 1, 1))
+        total = total + pltpu.roll(behind, 5, 0)
+        old = held.field[x, :, self.span(z)]
+        keep = held.keep[pl.ds(x * self.pitch + z, 1), :]
+        value = old - (self.component * keep) * (total + ground_spring * old)
+        self.store_node(refs, x, z, value, w_ref)
+
+    def sweep(self, level, layers, split_at, coefficients_at, carried, emit, carry_to):
+        for x in layers:
+            vol_ref, dev_ref = coefficients_at(x)
+            z, end = level - 1, self.size_z - level
+            side_low = side_high = None
+            while z < end:
+                cols = min(2, end - z)
+                lanes = cols * self.ny
+                parts = []
+                for a in (0, 1):
+                    source = split_at(x + a)
+                    for c in (0, 1):
+                        parts.append(source[x + a, :, (z + c) * self.ny : (z + c) * self.ny + lanes])
+                rhs = jnp.concatenate(parts + parts, axis=0)
+                forces = jnp.dot(self.kmat, rhs, preferred_element_type=jnp.float32)
+                for j in range(cols):
+                    here = z + j
+                    vol = vol_ref[pl.ds(x * self.pitch + here, 1), :]
+                    dev = dev_ref[pl.ds(x * self.pitch + here, 1), :]
+                    g = []
+                    for q in range(4):
+                        f_vol = forces[8 * q : 8 * q + 8, self.span(j)]
+                        f_dev = forces[32 + 8 * q : 40 + 8 * q, self.span(j)]
+                        g.append(vol * f_vol + dev * f_dev)
+                    if here >= level:
+                        before = None if carried is None else carried[:, self.span(here)]
+                        carry_to[:, self.span(here)] = g[2] + side_high
+                        emit(x, here, g[0] + side_low, before)
+                    side_low, side_high = g[1], g[3]
+                z += cols
+            carried = carry_to
+
+
+Refs = collections.namedtuple("Refs", ("vol", "dev", "keep", "field", "split"))
+
+
+def gram_tiles(nx, nz, here, w_at, sums):
+    for c in range(3):
+        for x in range(nx):
+            for t in range(nz // 8):
+                at = (c * nx + x) * nz + 8 * t
+                w = {}
+                for n, (i, j) in enumerate(PAIRS):
+                    if here(j, x):
+                        for level in (i, j):
+                            if level not in w:
+                                w[level] = w_at(level, x)[at : at + 8, :]
+                        term = w[i] * w[j]
+                        sums[n] = term if sums[n] is None else sums[n] + term
+    return sums
+
+
+def inner_product_kernel(
     dims,
-    load_ref, plastic_ref, modulus_ref, sa_ref, sb_ref, ca_ref, cb_ref, k_ref, scale_ref,
-    w0_ref, w1_ref, w2_ref, w3_ref, gram_ref,
-    slow_ref, shigh_ref, clow_ref, chigh_ref, vol_ref, dev_ref, keep_ref, field_ref, split_ref, sum_ref,
+    load_ref, plastic_ref, modulus_ref, ca_ref, cb_ref, k_ref, scale_ref,
+    w0_ref, w1_ref, w2_ref, w3_ref, part_ref, stash_ref,
+    vol_ref, dev_ref, keep_ref, field_ref, split_ref, clow_ref, chigh_ref,
+    sum_ref,
 ):
     nx, nz, ny, _, tz, _ = dims
-    size_x = nx + 2 * HALO
-    size_z = nz + 2 * HALO
-    pitch = round_up(size_z, 8)
+    work = Products(dims, k_ref[...], scale_ref)
+    pitch = work.pitch
+    refs = Refs(vol_ref, dev_ref, keep_ref, field_ref, split_ref)
     w_refs = (w0_ref, w1_ref, w2_ref, w3_ref)
-    pick(sa_ref, sb_ref, is_odd("sub"), slow_ref, shigh_ref)
     pick(ca_ref, cb_ref, is_odd("curve"), clow_ref, chigh_ref)
-
-    for x in range(size_x - 1):
-        row = x * pitch
-        if HALO <= x < HALO + nx:
-            own = x - HALO
-            dev_ref[row + HALO : row + HALO + nz, :] = plastic_ref[own * nz : (own + 1) * nz, :]
-            e_ref, e_row = modulus_ref, own // TILE * tz
-            rims = (clow_ref, 4 * HALO * nx + own // TILE), (chigh_ref, 4 * HALO * nx + own // TILE)
-        else:
-            side_ref, xl = (slow_ref, x) if x < HALO else (shigh_ref, x - HALO - nx)
-            at = (3 * HALO + xl) * size_z
-            dev_ref[row : row + size_z, :] = side_ref[at : at + size_z, :]
-            at = 4 * HALO * size_z
-            e_ref, e_row = side_ref, at + 1
-            rims = (side_ref, at), (side_ref, at + 1 + tz)
+    for own in range(nx):
+        row = (own + HALO) * pitch
+        dev_ref[row + HALO : row + HALO + nz, :] = plastic_ref[own * nz : (own + 1) * nz, :]
+        tile_x = own // TILE
         for t in range(tz):
-            value = jnp.broadcast_to(e_ref[e_row + t : e_row + t + 1, :], (TILE, ny))
+            value = modulus_ref[tile_x * tz + t : tile_x * tz + t + 1, :]
             first = row + HALO + t * TILE
-            vol_ref[first : first + TILE, :] = value
-        for (ref, at), first in zip(rims, (row, row + HALO + nz)):
+            vol_ref[first : first + TILE, :] = jnp.broadcast_to(value, (TILE, ny))
+        at = 4 * HALO * nx + tile_x
+        for ref, first in ((clow_ref, row), (chigh_ref, row + HALO + nz)):
             vol_ref[first : first + HALO, :] = jnp.broadcast_to(ref[at : at + 1, :], (HALO, ny))
     for zl in range(HALO):
         at = (3 * HALO + zl) * nx
         for ref, z in ((clow_ref, zl), (chigh_ref, HALO + nz + zl)):
             dev_ref[pl.ds(HALO * pitch + z, nx, stride=pitch), :] = ref[at : at + nx, :]
-    first_lane = lax.broadcasted_iota(jnp.int32, (8, ny), 1) == 0
-    last_lane = lax.broadcasted_iota(jnp.int32, (8, ny), 1) == ny - 1
-
-    x_index = lax.axis_index("sub") * nx - HALO
-    x_count = lax.axis_size("sub") * nx
-    z_row = lax.broadcasted_iota(jnp.int32, (pitch, ny), 0) + (lax.axis_index("curve") * nz - HALO)
-    z_free = (z_row > 0) & (z_row < lax.axis_size("curve") * nz)
-    y_free = lax.broadcasted_iota(jnp.int32, (pitch, ny), 1) > 0
-    free = (z_free & y_free).astype(jnp.float32)
-    row_index = lax.broadcasted_iota(jnp.int32, (pitch, ny), 0)
-    for x in range(size_x):
-        below = max(x - 1, 0) * pitch
-        above = min(x, size_x - 2) * pitch
-        e = jnp.maximum(vol_ref[below : below + pitch, :], vol_ref[above : above + pitch, :])
-        e = jnp.where(row_index < size_z - 1, e, pltpu.roll(e, 1, 0))
-        before = jnp.where(row_index == 0, e, pltpu.roll(e, 1, 0))
-        e = jnp.maximum(e, before)
-        e = jnp.maximum(e, pltpu.roll(e, 1, 1))
-        here = x_index + x
-        x_free = jnp.where((here > 0) & (here < x_count), 1.0, 0.0)
-        keep_ref[x * pitch : (x + 1) * pitch, :] = jnp.where(e > 0, free * x_free, 0.0)
+    first, last = HALO + 1, HALO + nx - 1
+    work.mark_kept(refs, range(first, last + 1), lambda x: vol_ref)
+    for own in range(nx):
+        work.deviatoric(refs, own + HALO)
+    for x in range(first, last + 1):
+        own = x - HALO
+        for z in range(work.size_z):
+            if z < HALO:
+                rows = clow_ref[pl.ds(z * nx + own, 3, stride=HALO * nx), :]
+            elif z >= HALO + nz:
+                rows = chigh_ref[pl.ds((z - HALO - nz) * nx + own, 3, stride=HALO * nx), :]
+            else:
+                rows = load_ref[pl.ds(own * nz + z - HALO, 3, stride=nx * nz), :]
+            work.start_node(refs, x, z, rows, w0_ref)
+    for level in range(1, ITERS + 1):
+        layers = range(HALO + level, HALO + nx - level)
+        low_ref, high_ref = stash_ref.at[2 * level - 2], stash_ref.at[2 * level - 1]
+
+        def emit(x, z, total, before, level=level, low_ref=low_ref):
+            if before is None:
+                low_ref[:, work.span(z)] = total
+            else:
+                work.update_node(refs, refs, x, z, total + before, w_refs[level])
+
+        work.sweep(
+            level, layers[:-1], lambda x: split_ref, lambda x: (vol_ref, dev_ref), None, emit, sum_ref
+        )
+        carried = sum_ref if len(layers) > 1 else None
+        work.sweep(
+            level, layers[-1:], lambda x: split_ref, lambda x: (vol_ref, dev_ref), carried, emit, high_ref
+        )
+    sums = gram_tiles(
+        nx, nz, lambda j, x: x in inner_rows(nx, j), lambda j, x: w_refs[j], [None] * len(PAIRS)
+    )
+    for n, value in enumerate(sums):
+        part_ref[8 * n : 8 * n + 8, :] = jnp.zeros((8, ny), jnp.float32) if value is None else value
+
+
+def outer_product_kernel(
+    dims,
+    modulus_ref, load_ref, sa_ref, sb_ref, k_ref, scale_ref,
+    a0_ref, a1_ref, a2_ref, a3_ref, part_ref, stash_ref,
+    ivol_ref, idev_ref, ikeep_ref, ifield_ref, isplit_ref, clow_ref, chigh_ref,
+    b0_ref, b1_ref, b2_ref, b3_ref, gram_ref,
+    slow_ref, shigh_ref, vol_ref, dev_ref, keep_ref, field_ref, split_ref, sum_ref,
+):
+    nx, nz, ny, _, tz, _ = dims
+    work = Products(dims, k_ref[...], scale_ref)
+    pitch, size_x, size_z = work.pitch, work.size_x, work.size_z
+    refs = Refs(vol_ref, dev_ref, keep_ref, field_ref, split_ref)
+    inner = Refs(ivol_ref, idev_ref, ikeep_ref, ifield_ref, isplit_ref)
+    a_refs = (a0_ref, a1_ref, a2_ref, a3_ref)
+    b_refs = (b0_ref, b1_ref, b2_ref, b3_ref)
+    pick(sa_ref, sb_ref, is_odd("sub"), slow_ref, shigh_ref)
+    own_layers = range(HALO, HALO + nx)
     for x in range(size_x - 1):
-        rows = pl.ds(x * pitch, pitch)
-        dev_ref[rows, :] = vol_ref[rows, :] * (1.0 - dev_ref[rows, :])
-
-    def store_node(x, z, value):
-        ahead = jnp.where(last_lane, 0.0, pltpu.roll(value, ny - 1, 1))
-        both = value + pltpu.roll(ahead, 3, 0)
-        field_ref[x, :, z * ny : (z + 1) * ny] = value
-        high = both.astype(jnp.bfloat16).astype(jnp.float32)
-        split_ref[x, :, z * ny : (z + 1) * ny] = jnp.concatenate([high, both - high], axis=0).astype(jnp.bfloat16)
-
-    blank = jnp.zeros((5, ny), jnp.float32)
-    for x in range(size_x):
+        if x in own_layers:
+            continue
+        row = x * pitch
+        side_ref, xl = (slow_ref, x) if x < HALO else (shigh_ref, x - HALO - nx)
+        at = (3 * HALO + xl) * size_z
+        dev_ref[row : row + size_z, :] = side_ref[at : at + size_z, :]
+        at = 4 * HALO * size_z
+        for t in range(tz):
+            first = row + HALO + t * TILE
+            value = side_ref[at + 1 + t : at + 2 + t, :]
+            vol_ref[first : first + TILE, :] = jnp.broadcast_to(value, (TILE, ny))
+        for rim, first in ((at, row), (at + 1 + tz, row + HALO + nz)):
+            vol_ref[first : first + HALO, :] = jnp.broadcast_to(side_ref[rim : rim + 1, :], (HALO, ny))
+    started = range(HALO + 1, HALO + nx)
+    rest = [x for x in range(size_x) if x not in started]
+    work.mark_kept(refs, rest, lambda x: ivol_ref if x in own_layers else vol_ref)
+    for x in range(size_x - 1):
+        if x not in own_layers:
+            work.deviatoric(refs, x)
+    for x in rest:
         for z in range(size_z):
             if x < HALO:
                 rows = slow_ref[pl.ds(x * size_z + z, 3, stride=HALO * size_z), :]
@@ -213,63 +370,46 @@
                 rows = chigh_ref[pl.ds((z - HALO - nz) * nx + x - HALO, 3, stride=HALO * nx), :]
             else:
                 rows = load_ref[pl.ds((x - HALO) * nz + z - HALO, 3, stride=nx * nz), :]
-            value = jnp.concatenate([rows, blank], axis=0) * keep_ref[pl.ds(x * pitch + z, 1), :]
-            store_node(x, z, value)
-
-    def save(out_ref):
-        for x in range(nx):
-            for z in range(nz):
-                value = field_ref[x + HALO, 0:3, (z + HALO) * ny : (z + HALO + 1) * ny]
-                out_ref[pl.ds(x * nz + z, 3, stride=nx * nz), :] = value
-
-    save(w0_ref)
-    kmat = k_ref[...]
-    inverse = scale_ref[0:1, 0:1]
-    component = (lax.broadcasted_iota(jnp.int32, (8, ny), 0) < 3).astype(jnp.float32) * inverse
-
-    for k in range(1, ITERS + 1):
-        sum_ref[...] = jnp.zeros_like(sum_ref)
-
-        for i in range(k - 1, size_x - k):
-            z = k - 1
-            end = size_z - k
-            side_low = side_high = None
-            while z < end:
-                cols = min(2, end - z)
-                lanes = cols * ny
-                parts = []
-                for a in (0, 1):
-                    for c in (0, 1):
-                        parts.append(split_ref[i + a, :, (z + c) * ny : (z + c) * ny + lanes])
-                rhs = jnp.concatenate(parts + parts, axis=0)
-                forces = jnp.dot(kmat, rhs, preferred_element_type=jnp.float32)
-                for j in range(cols):
-                    here = z + j
-                    vol = vol_ref[pl.ds(i * pitch + here, 1), :]
-                    dev = dev_ref[pl.ds(i * pitch + here, 1), :]
-                    g = []
-                    for q in range(4):
-                        f_vol = forces[8 * q : 8 * q + 8, j * ny : (j + 1) * ny]
-                        f_dev = forces[32 + 8 * q : 40 + 8 * q, j * ny : (j + 1) * ny]
-                        g.append(vol * f_vol + dev * f_dev)
-                    if here >= k:
-                        span = slice(here * ny, (here + 1) * ny)
-                        total = sum_ref[:, span] + (g[0] + side_low)
-                        sum_ref[:, span] = g[2] + side_high
-                        behind = jnp.where(first_lane, 0.0, pltpu.roll(total, 1, 1))
-                        total = total + pltpu.roll(behind, 5, 0)
-                        old = field_ref[i, :, span]
-                        keep = keep_ref[pl.ds(i * pitch + here, 1), :]
-                        store_node(i, here, old - (component * keep) * (total + ground_spring * old))
-                    side_low, side_high = g[1], g[3]
-                z += cols
-        save(w_refs[k])
-
-    sums = [jnp.zeros((8, ny), jnp.float32) for _ in PAIRS]
-    for r in range(3 * nx * nz // 8):
-        w = [ref[8 * r : 8 * r + 8, :] for ref in w_refs]
-        for n, (i, j) in enumerate(PAIRS):
-            sums[n] = sums[n] + w[i] * w[j]
+            work.start_node(refs, x, z, rows, b0_ref)
+
+    held = {x: inner if x in started else refs for x in range(size_x)}
+    keeps = dict(held)
+
+    def update(x, z, total, level):
+        source = keeps[x]._replace(field=held[x].field)
+        work.update_node(refs, source, x, z, total, b_refs[level])
+
+    def coefficients_at(x):
+        source = inner if x in own_layers else refs
+        return source.vol, source.dev
+
+    for level in range(1, ITERS + 1):
+        done = []
+
+        def emit(x, z, total, before, level=level, done=done):
+            if before is not None:
+                update(x, z, total + before, level)
+                done.append(x)
+
+        def split_at(x):
+            return held[x].split
+
+        edge = HALO + level
+        work.sweep(level, range(level - 1, edge), split_at, coefficients_at, None, emit, sum_ref)
+        low_ref, high_ref = stash_ref.at[2 * level - 2], stash_ref.at[2 * level - 1]
+        for z in range(level, size_z - level):
+            update(edge, z, sum_ref[:, work.span(z)] + low_ref[:, work.span(z)], level)
+        done.append(edge)
+        upper = range(HALO + nx - level, size_x - level)
+        work.sweep(level, upper, split_at, coefficients_at, high_ref, emit, sum_ref)
+        for x in set(done):
+            held[x] = refs
+
+    sums = [part_ref[8 * n : 8 * n + 8, :] for n in range(len(PAIRS))]
+    sums = gram_tiles(
+        nx, nz, lambda j, x: x not in inner_rows(nx, j),
+        lambda j, x: (a_refs if x in inner_rows(nx, j) else b_refs)[j], sums,
+    )
     lane = lax.broadcasted_iota(jnp.int32, (1, ny), 1)
     row = jnp.zeros((1, ny), jnp.float32)
     for n, value in enumerate(sums):
@@ -277,7 +417,10 @@
     gram_ref[...] = jnp.broadcast_to(row[None], gram_ref.shape)
 
 
-def finish_kernel(gram_ref, scale_ref, w0_ref, w1_ref, w2_ref, w3_ref, solution_ref, residual_ref, better_ref, poor_ref):
+def finish_kernel(dims, gram_ref, scale_ref, *refs):
+    nx, nz = dims[:2]
+    a_refs, b_refs = refs[: ITERS + 1], refs[ITERS + 1 : 2 * ITERS + 2]
+    solution_ref, residual_ref, better_ref, poor_ref = refs[2 * ITERS + 2 :]
     total = jnp.sum(gram_ref[...], axis=0)
     lane = lax.broadcasted_iota(jnp.int32, total.shape, 1)
     gram = {}
@@ -336,14 +479,17 @@
             norm_now = norm_next
     inverse = scale_ref[0:1, 0:1]
     better_ref[...] = jnp.broadcast_to(first_step * inverse, better_ref.shape)
-    w_refs = (w0_ref, w1_ref, w2_ref, w3_ref)
     solution = [None if c is None else c * inverse for c in solution]
-    for out_ref, coefs in ((solution_ref, solution), (residual_ref, residual)):
-        value = None
-        for c, ref in zip(coefs, w_refs):
-            if c is not None:
-                value = c * ref[...] if value is None else value + c * ref[...]
-        out_ref[...] = value
+    for x in range(nx):
+        for component in range(3):
+            rows = slice((component * nx + x) * nz, (component * nx + x + 1) * nz)
+            w = [(a_refs if x in inner_rows(nx, j) else b_refs)[j][rows, :] for j in range(ITERS + 1)]
+            for out_ref, coefs in ((solution_ref, solution), (residual_ref, residual)):
+                value = None
+                for c, vector in zip(coefs, w):
+                    if c is not None:
+                        value = c * vector if value is None else value + c * vector
+                out_ref[rows, :] = value
     terms = None
     for i, c in enumerate(residual):
         size = jnp.abs(c) * jnp.sqrt(gram[i, i])
@@ -361,9 +507,13 @@
     smem = pl.BlockSpec(memory_space=pltpu.SMEM)
     shape = jax.ShapeDtypeStruct
     kept = pltpu.VMEM
+    grant = pltpu.CompilerParams(vmem_limit_bytes=16 * 2**20)
 
     def near(*values):
         return [pltpu.with_memory_space_constraint(v, pltpu.VMEM) for v in values]
+
+    def far(*values):
+        return [pltpu.with_memory_space_constraint(v, pltpu.HBM) for v in values]
 
     load = load.reshape(3 * nx * nz, ny)
     plastic = plastic.reshape(nx * nz, ny)
@@ -379,15 +529,17 @@
         out_shape=(kept((curve_rows, ny), f32), kept((curve_rows, ny), f32), kept((round_up(tx * tz, 8), ny), f32)),
         in_specs=[smem, smem, vmem, vmem],
         out_specs=(vmem,) * 3,
+        compiler_params=grant,
         name="curve_message",
-    )(tile_material, moduli, load, plastic)
+    )(*far(tile_material, moduli, load, plastic))
     k_both, scale = pl.pallas_call(
         setup_kernel,
         out_shape=(kept((64, 128), jnp.bfloat16), kept((8, 128), f32)),
         in_specs=[smem, vmem, vmem, vmem],
         out_specs=(vmem,) * 2,
+        compiler_params=grant,
         name="setup",
-    )(moduli, k_vol, k_dev, *near(modulus))
+    )(*far(moduli), k_vol, k_dev, *near(modulus))
     curve_b = exchange(curve_b, "curve", 1)
     curve_a = exchange(curve_a, "curve", 0)
     sub_a, sub_b = pl.pallas_call(
@@ -396,36 +548,58 @@
         in_specs=[vmem] * 6,
         out_specs=(vmem,) * 2,
         scratch_shapes=[pltpu.VMEM((curve_rows, ny), f32)] * 2,
+        compiler_params=grant,
         name="sub_message",
     )(*near(load, plastic, modulus, curve_a, curve_b, scale))
     sub_b = exchange(sub_b, "sub", 1)
     sub_a = exchange(sub_a, "sub", 0)
+    basis_shape = (kept((3 * nx * nz, ny), f32),) * (ITERS + 1)
+    coefficient = (size_x * pitch, ny)
+    field = (size_x, 8, size_z * ny)
+    split = (size_x, 16, size_z * ny)
+    stash = (2 * ITERS, 8, size_z * ny)
 
     def solve(scale):
-        *basis, gram = pl.pallas_call(
-            functools.partial(product_kernel, dims),
-            out_shape=(kept((3 * nx * nz, ny), f32),) * (ITERS + 1) + (kept((count, 1, ny), f32),),
-            in_specs=[vmem] * 9,
+        *first, part, stashed, vol, dev, keep, fields, splits, low, high = pl.pallas_call(
+            functools.partial(inner_product_kernel, dims),
+            out_shape=basis_shape + (
+                kept((8 * len(PAIRS), ny), f32), kept(stash, f32),
+                kept(coefficient, f32), kept(coefficient, f32), kept(coefficient, f32),
+                kept(field, f32), kept(split, jnp.bfloat16),
+                kept((curve_rows, ny), f32), kept((curve_rows, ny), f32),
+            ),
+            in_specs=[vmem] * 7,
+            out_specs=(vmem,) * (ITERS + 10),
+            scratch_shapes=[pltpu.VMEM((8, size_z * ny), f32)],
+            compiler_params=grant,
+            name="inner_products",
+        )(*near(load, plastic, modulus, curve_a, curve_b, k_both, scale))
+        *second, gram = pl.pallas_call(
+            functools.partial(outer_product_kernel, dims),
+            out_shape=basis_shape + (kept((count, 1, ny), f32),),
+            in_specs=[vmem] * (ITERS + 16),
             out_specs=(vmem,) * (ITERS + 2),
             scratch_shapes=[
                 pltpu.VMEM((sub_rows, ny), f32), pltpu.VMEM((sub_rows, ny), f32),
-                pltpu.VMEM((curve_rows, ny), f32), pltpu.VMEM((curve_rows, ny), f32),
-                pltpu.VMEM((size_x * pitch, ny), f32), pltpu.VMEM((size_x * pitch, ny), f32),
-                pltpu.VMEM((size_x * pitch, ny), f32),
-                pltpu.VMEM((size_x, 8, size_z * ny), f32),
-                pltpu.VMEM((size_x, 16, size_z * ny), jnp.bfloat16),
+                pltpu.VMEM(coefficient, f32), pltpu.VMEM(coefficient, f32), pltpu.VMEM(coefficient, f32),
+                pltpu.VMEM(field, f32), pltpu.VMEM(split, jnp.bfloat16),
                 pltpu.VMEM((8, size_z * ny), f32),
             ],
-            name="products",
-        )(*near(load, plastic, modulus, sub_a, sub_b, curve_a, curve_b, k_both, scale))
+            compiler_params=grant,
+            name="outer_products",
+        )(*near(
+            modulus, load, sub_a, sub_b, k_both, scale,
+            *first, part, stashed, vol, dev, keep, fields, splits, low, high,
+        ))
         gram = lax.all_to_all(gram, AXES, 0, 0)
         return pl.pallas_call(
-            finish_kernel,
+            functools.partial(finish_kernel, dims),
             out_shape=(shape((3 * nx * nz, ny), f32),) * 2 + (kept((8, 128), f32), pltpu.SMEM((1, 1), jnp.int32)),
-            in_specs=[vmem] * 6,
+            in_specs=[vmem] * (2 * ITERS + 4),
             out_specs=(vmem, vmem, vmem, smem),
+            compiler_params=grant,
             name="finish",
-        )(*near(gram, scale, *basis))
+        )(*near(gram, scale, *first, *second))
 
     *found, better, poor = solve(scale)
     found = lax.cond(poor[0, 0] > 0, lambda: tuple(solve(better)[:2]), lambda: tuple(found))

time: 34.9 us -> 33.2 us (0.951)
  blocking collectives: 21.3 us -> 19.9 us
  waiting for transfers between devices: 0.94 us -> 0.39 us
    all_to_all x1, blocking collectives: 21.3 us -> 19.9 us  [solve(): gram = lax.all_to_all(gram, AXES, 0, 0)]
    ppermute x4, waiting for transfers between devices: 0.94 us -> 0.39 us  [exchange(): return lax.ppermute(value, axis, pairs)]
    pallas_call x2 -> x3, Pallas kernels: 5.04 us -> 5.4 us  [the longest x1 2.55 us: solve(): pl.pallas_call(functools.partial(outer_product_kernel, dims), out_shape=b...]
  transfers between devices with their start and end apart: 4 -> 4, of which waited for: 2 -> 1; matrix products, arithmetic and copies ran while one was open for 0% -> 0% of each run, Pallas kernels for 3% -> 9%
where the time goes in v5:
time: 33.2 us; the launch traced here: 33 us
  blocking collectives  19.9 us (60%)
  Pallas kernels  7.54 us (23%)
  starting transfers between devices  4.42 us (13%)
  between operations  0.75 us (2%)
  waiting for transfers between devices  0.39 us (1%)
    all_to_all x1, blocking collectives, solve(): gram = lax.all_to_all(gram, AXES, 0, 0)  19.9 us
    ppermute x4, starting transfers between devices, exchange(): return lax.ppermute(value, axis, pairs)  4.42 us
    pallas_call x1, Pallas kernels, solve(): pl.pallas_call(functools.partial(outer_product_kernel, dims), out_shape=b...  2.55 us
    pallas_call x1, Pallas kernels, solve(): pl.pallas_call(functools.partial(inner_product_kernel, dims), out_shape=b...  1.96 us
    pallas_call x1, Pallas kernels, local(): pl.pallas_call(setup_kernel, out_shape=(kept((64, 128), jnp.bfloat16), ke...  1.05 us
    pallas_call x1, Pallas kernels, local(): pl.pallas_call(functools.partial(curve_message_kernel, dims), out_shape=(...  1.03 us
    pallas_call x1, Pallas kernels, solve(): pl.pallas_call(functools.partial(finish_kernel, dims), out_shape=(shape((...  0.89 us
  transfers between devices with their start and end apart: 4, of which 1 were waited for; matrix products, arithmetic and copies ran while one was open for 0% of the time, Pallas kernels for 9%

profile of v5, /device:TPU:0, one launch (start us, length us, event | category | flops | bytes accessed | tf_op | source)
XLA Modules:
  0.0 33.0 jit_solution(17685485687816421838)
XLA Ops:
  0.6 0.0 copy-start
  0.6 0.0 copy-start.2
  0.7 0.0 copy-start.3
  0.7 1.0 %curve_message.1 = (f32[104,128]{1,0:T(8,128)S(1)}, f32[104,128]{1,0:T(8,128)S(1)}, f32[8,128]{1,0:T(8,128)S(1)}) custom-call(s32[1,1,16]{2,1,0:T(1,128)} %tile_ref.1, f32[4]{0:T(128)} %moduli_ref.3, f32[192,128]{1,0:T(8,128)} %bitcast.7, f32[64,128]{1,0:T(8,128)} %bitcast.12), custom_call_target="tpu_custom_call" | custom-call | tf_op jit(solution)/shard_map/curve_message/pallas_call | solution.py:527
  1.7 0.0 copy-start.1
  1.7 3.0 %collective-permute-start = (f32[104,128]{1,0:T(8,128)S(1)}, f32[104,128]{1,0:T(8,128)S(1)}, u32[]{:S(2)}, u32[]{:S(2)}) collective-permute-start(f32[104,128]{1,0:T(8,128)S(1)} %get-tuple-element.89), channel_id=1, source_target_pairs={{0,4},{4,0},{8,12},{12,8},{16,20},{20,16},{24,28},{28,24},{1,5},{5... | collective-permute-start | bytes 159752 | tf_op jit(solution)/shard_map/ppermute | solution.py:33
  4.7 0.7 %collective-permute-start.1 = (f32[104,128]{1,0:T(8,128)S(1)}, f32[104,128]{1,0:T(8,128)S(1)}, u32[]{:S(2)}, u32[]{:S(2)}) collective-permute-start(f32[104,128]{1,0:T(8,128)S(1)} %get-tuple-element.90), channel_id=1, source_target_pairs={{4,8},{8,4},{12,16},{16,12},{20,24},{24,20},{5,9},{9,5},{13,17},{1... | collective-permute-start | bytes 159752 | tf_op jit(solution)/shard_map/ppermute | solution.py:33
  5.4 0.0 copy-done.2
  5.4 0.0 copy-done.3
  5.4 1.0 %setup.1 = (bf16[64,128]{1,0:T(8,128)(2,1)S(1)}, f32[8,128]{1,0:T(8,128)S(1)}) custom-call(f32[4]{0:T(128)} %moduli_ref.3, f32[24,24]{1,0:T(8,128)S(1)} %copy-done.2, f32[24,24]{1,0:T(8,128)S(1)} %copy-done.3, f32[8,128]{1,0:T(8,128)S(1)} %get-tuple-element.88._.modulus_ref), custom_call_target="tpu_custom_call" | custom-call | tf_op jit(solution)/shard_map/setup/pallas_call | solution.py:535
  6.5 0.4 %collective-permute-done.ra_ref.ca_ref = f32[104,128]{1,0:T(8,128)S(1)} collective-permute-done((f32[104,128]{1,0:T(8,128)S(1)}, f32[104,128]{1,0:T(8,128)S(1)}, u32[]{:S(2)}, u32[]{:S(2)}) %collective-permute-start) | collective-permute-done | bytes 53280 | tf_op jit(solution)/shard_map/ppermute | solution.py:33
  6.9 0.0 collective-permute-done.1.rb_ref.cb_ref
  6.9 0.0 copy-done
  6.9 0.0 copy-done.1
  6.9 0.1 sub_message.1
  6.9 0.1 collective-permute-start.2
  7.0 0.7 %collective-permute-start.3 = (f32[176,128]{1,0:T(8,128)S(1)}, f32[176,128]{1,0:T(8,128)S(1)}, u32[]{:S(2)}, u32[]{:S(2)}) collective-permute-start(f32[176,128]{1,0:T(8,128)S(1)} %get-tuple-element.93), channel_id=1, source_target_pairs={{1,2},{2,1},{5,6},{6,5},{9,10},{10,9},{13,14},{14,13},{17,18},{18,... | collective-permute-start | bytes 270344 | tf_op jit(solution)/shard_map/ppermute | solution.py:33
  7.7 2.0 %inner_products.3 = (f32[192,128]{1,0:T(8,128)S(1)}, f32[192,128]{1,0:T(8,128)S(1)}, f32[192,128]{1,0:T(8,128)S(1)}, f32[192,128]{1,0:T(8,128)S(1)}, f32[80,128]...) custom-call(f32[192,128]{1,0:T(8,128)S(1)} %bitcast.9, ...), custom_call_target="tpu_custom_call" | custom-call | tf_op jit(solution)/shard_map/inner_products/pallas_call | solution.py:563
  9.6 0.0 collective-permute-done.2.sa_ref
  9.7 0.0 collective-permute-done.3.sb_ref
  9.7 2.5 %outer_products.3 = (f32[192,128]{1,0:T(8,128)S(1)}, f32[192,128]{1,0:T(8,128)S(1)}, f32[192,128]{1,0:T(8,128)S(1)}, f32[192,128]{1,0:T(8,128)S(1)}, f32[32,1,128]{2,1,0:T(1,128)S(1)}) custom-call(f32[8,128]{1,0:T(8,128)S(1)} %get-tuple-element.88._.modulus_ref, f32[192,128]{1,0:T(8,128)S(1)} %bitcast.10, f32[176,128]{1,0:T(8,128)S(1)} %collective-permute-done.2.sa_ref, ...), custom_call_target="tpu_custom_call" | custom-call | tf_op jit(solution)/shard_map/outer_products/pallas_call | solution.py:577
  12.2 19.9 %all_to_all.10.gram_ref = f32[32,1,128]{2,1,0:T(1,128)S(1)} all-to-all(f32[32,1,128]{2,1,0:T(1,128)S(1)} %get-tuple-element.108), channel_id=1, replica_groups=mesh['curve'=8,'sub'=4] {'curve','sub'}, dimensions={0} | all-to-all | bytes 32768 | tf_op jit(solution)/shard_map/all_to_all | solution.py:594
  32.1 0.9 %finish.3 = (f32[192,128]{1,0:T(8,128)}, f32[192,128]{1,0:T(8,128)}, f32[8,128]{1,0:T(8,128)S(1)}, s32[1,1]{1,0:T(1,128)S(4)}) custom-call(f32[32,1,128]{2,1,0:T(1,128)S(1)} %all_to_all.10.gram_ref, f32[8,128]{1,0:T(8,128)S(1)} %get-tuple-element.91._.scale_ref, f32[192,128]{1,0:T(8,128)S(1)} %get-tuple-element.95.a0_ref.refs_0_, ...), custom_call_target="tpu_custom_call" | custom-call | tf_op jit(solution)/shard_map/finish/pallas_call | solution.py:595
  (1 shorter events, 0.0 us)
Async XLA Ops:
  0.6 6.2 %copy-start = (f32[3,8,8,128]{3,2,1,0:T(8,128)S(1)}, f32[3,8,8,128]{3,2,1,0:T(8,128)}, u32[]{:S(2)}) copy-start(f32[3,8,8,128]{3,2,1,0:T(8,128)} %param.8) | copy-start | bytes 294916
  0.6 4.8 %copy-start.2 = (f32[24,24]{1,0:T(8,128)S(1)}, f32[24,24]{1,0:T(8,128)}, u32[]{:S(2)}) copy-start(f32[24,24]{1,0:T(8,128)} %kv_ref.1) | copy-start | bytes 6916
  0.7 4.8 %copy-start.3 = (f32[24,24]{1,0:T(8,128)S(1)}, f32[24,24]{1,0:T(8,128)}, u32[]{:S(2)}) copy-start(f32[24,24]{1,0:T(8,128)} %kd_ref.1) | copy-start | bytes 6916
  1.7 5.2 %copy-start.1 = (f32[8,8,128]{2,1,0:T(8,128)S(1)}, f32[8,8,128]{2,1,0:T(8,128)}, u32[]{:S(2)}) copy-start(f32[8,8,128]{2,1,0:T(8,128)} %param.9) | copy-start | bytes 98308
  1.7 5.1 %collective-permute-start = (f32[104,128]{1,0:T(8,128)S(1)}, f32[104,128]{1,0:T(8,128)S(1)}, u32[]{:S(2)}, u32[]{:S(2)}) collective-permute-start(f32[104,128]{1,0:T(8,128)S(1)} %get-tuple-element.89), channel_id=1, source_target_pairs={{0,4},{4,0},{8,12},{12,8},{16,20},{20,16},{24,28},{28,24},{1,5},{5... | collective-permute-start | bytes 159752 | tf_op jit(solution)/shard_map/ppermute | solution.py:33
  4.7 2.1 %collective-permute-start.1 = (f32[104,128]{1,0:T(8,128)S(1)}, f32[104,128]{1,0:T(8,128)S(1)}, u32[]{:S(2)}, u32[]{:S(2)}) collective-permute-start(f32[104,128]{1,0:T(8,128)S(1)} %get-tuple-element.90), channel_id=1, source_target_pairs={{4,8},{8,4},{12,16},{16,12},{20,24},{24,20},{5,9},{9,5},{13,17},{1... | collective-permute-start | bytes 159752 | tf_op jit(solution)/shard_map/ppermute | solution.py:33
  6.9 2.7 %collective-permute-start.2 = (f32[176,128]{1,0:T(8,128)S(1)}, f32[176,128]{1,0:T(8,128)S(1)}, u32[]{:S(2)}, u32[]{:S(2)}) collective-permute-start(f32[176,128]{1,0:T(8,128)S(1)} %get-tuple-element.92), channel_id=1, source_target_pairs={{0,1},{1,0},{2,3},{3,2},{4,5},{5,4},{6,7},{7,6},{8,9},{9,8},{10,11... | collective-permute-start | bytes 270344 | tf_op jit(solution)/shard_map/ppermute | solution.py:33
  7.0 2.6 %collective-permute-start.3 = (f32[176,128]{1,0:T(8,128)S(1)}, f32[176,128]{1,0:T(8,128)S(1)}, u32[]{:S(2)}, u32[]{:S(2)}) collective-permute-start(f32[176,128]{1,0:T(8,128)S(1)} %get-tuple-element.93), channel_id=1, source_target_pairs={{1,2},{2,1},{5,6},{6,5},{9,10},{10,9},{13,14},{14,13},{17,18},{18,... | collective-permute-start | bytes 270344 | tf_op jit(solution)/shard_map/ppermute | solution.py:33

commit v6 on v5

--- a/solution.py
+++ b/solution.py
@@ -143,69 +143,84 @@
         self.size_z = self.nz + 2 * HALO
         self.pitch = round_up(self.size_z, 8)
         self.kmat = kmat
-        lane = lax.broadcasted_iota(jnp.int32, (8, self.ny), 1)
-        self.first_lane = lane == 0
-        self.last_lane = lane == self.ny - 1
-        rows = lax.broadcasted_iota(jnp.int32, (8, self.ny), 0)
-        self.component = (rows < 3).astype(jnp.float32) * scale_ref[0:1, 0:1]
+        self.component = lax.broadcasted_iota(jnp.int32, (8, self.ny), 0) < 3
+        self.inverse = scale_ref[0:1, 0:1]
         self.blank = jnp.zeros((5, self.ny), jnp.float32)
 
     def span(self, z):
         return slice(z * self.ny, (z + 1) * self.ny)
 
-    def deviatoric(self, refs, x):
-        rows = slice(x * self.pitch, (x + 1) * self.pitch)
-        refs.dev[rows, :] = refs.vol[rows, :] * (1.0 - refs.dev[rows, :])
-
-    def mark_kept(self, refs, layers, vol_at):
-        pitch, shape = self.pitch, (self.pitch, self.ny)
+    def tile(self, index):
+        return (index // TILE + 1)
+
+    def tile_row(self, x, z):
+        return self.tile(x - HALO) * (self.nz // TILE + 2) + self.tile(z - HALO)
+
+    def node_class(self, index):
+        return self.tile(index - HALO - 1), self.tile(index - HALO)
+
+    def mark_kept(self, refs, layers):
+        self.rows = {}
+        rows = refs.tiles.shape[0]
+        lane = lax.broadcasted_iota(jnp.int32, (1, self.ny), 1)
+        own, ahead = [], []
+        for at in range(0, rows, 8):
+            e = refs.tiles[at : at + 8, :]
+            own.append(jnp.maximum(e, pltpu.roll(e, 1, 1)))
+            ahead.append(jnp.maximum(e, pltpu.roll(e, self.ny - 1, 1)))
+        own = jnp.concatenate(own, axis=0)
+        ahead = jnp.concatenate(ahead, axis=0)
+        per_x = self.nz // TILE + 2
         x_index = lax.axis_index("sub") * self.nx - HALO
         x_count = lax.axis_size("sub") * self.nx
-        z_row = lax.broadcasted_iota(jnp.int32, shape, 0)
-        z_index = z_row + (lax.axis_index("curve") * self.nz - HALO)
-        y_free = lax.broadcasted_iota(jnp.int32, shape, 1) > 0
-        free = (z_index > 0) & (z_index < lax.axis_size("curve") * self.nz) & y_free
-        free = free.astype(jnp.float32)
+        z_index = lax.axis_index("curve") * self.nz - HALO
+        z_count = lax.axis_size("curve") * self.nz
         for x in layers:
-            below = max(x - 1, 0)
-            above = min(x, self.size_x - 2)
-            e = jnp.maximum(
-                vol_at(below)[below * pitch : (below + 1) * pitch, :],
-                vol_at(above)[above * pitch : (above + 1) * pitch, :],
-            )
-            e = jnp.where(z_row < self.size_z - 1, e, pltpu.roll(e, 1, 0))
-            e = jnp.maximum(e, jnp.where(z_row == 0, e, pltpu.roll(e, 1, 0)))
-            e = jnp.maximum(e, pltpu.roll(e, 1, 1))
-            here = x_index + x
-            x_free = jnp.where((here > 0) & (here < x_count), 1.0, 0.0)
-            refs.keep[x * pitch : (x + 1) * pitch, :] = jnp.where(e > 0, free * x_free, 0.0)
-
-    def store_node(self, refs, x, z, value, w_ref):
-        ny, span = self.ny, self.span(z)
-        ahead = jnp.where(self.last_lane, 0.0, pltpu.roll(value, ny - 1, 1))
-        both = value + pltpu.roll(ahead, 3, 0)
-        refs.field[x, :, span] = value
+            for z in range(self.size_z):
+                key = self.node_class(x), self.node_class(z)
+                if key in self.rows:
+                    continue
+                n = self.rows[key] = len(self.rows)
+                free = (x_index + x > 0) & (x_index + x < x_count) & (z_index + z > 0) & (z_index + z < z_count)
+                free = jnp.where(free, 1.0, 0.0)
+                around = sorted({tx * per_x + tz for tx in key[0] for tz in key[1]})
+                kept = []
+                for e, inside in ((own, lane > 0), (ahead, lane < self.ny - 1)):
+                    top = functools.reduce(jnp.maximum, [e[r : r + 1, :] for r in around])
+                    kept.append(jnp.where(inside & (top > 0), free, 0.0))
+                refs.keep[n : n + 1, :] = kept[0]
+                refs.gain[n : n + 1, :] = kept[0] * self.inverse
+                refs.ahead[n : n + 1, :] = kept[1] * self.inverse
+
+    def kept_row(self, ref, x, z):
+        n = self.rows[self.node_class(x), self.node_class(z)]
+        return ref[n : n + 1, :]
+
+    def store_node(self, refs, x, z, both, w_ref):
+        span = self.span(z)
+        refs.field[x, :, span] = both
         high = both.astype(jnp.bfloat16).astype(jnp.float32)
         refs.split[x, :, span] = jnp.concatenate([high, both - high], axis=0).astype(jnp.bfloat16)
         own_x, own_z = x - HALO, z - HALO
         if 0 <= own_x < self.nx and 0 <= own_z < self.nz:
-            w_ref[pl.ds(own_x * self.nz + own_z, 3, stride=self.nx * self.nz), :] = value[0:3, :]
+            w_ref[pl.ds(own_x * self.nz + own_z, 3, stride=self.nx * self.nz), :] = both[0:3, :]
 
     def start_node(self, refs, x, z, rows, w_ref):
-        keep = refs.keep[pl.ds(x * self.pitch + z, 1), :]
-        self.store_node(refs, x, z, jnp.concatenate([rows, self.blank], axis=0) * keep, w_ref)
+        value = jnp.concatenate([rows, self.blank], axis=0) * self.kept_row(refs.keep, x, z)
+        ahead = pltpu.roll(pltpu.roll(value, self.ny - 1, 1), 3, 0)
+        self.store_node(refs, x, z, value + ahead, w_ref)
 
     def update_node(self, refs, held, x, z, total, w_ref):
-        behind = jnp.where(self.first_lane, 0.0, pltpu.roll(total, 1, 1))
-        total = total + pltpu.roll(behind, 5, 0)
+        below = pltpu.roll(pltpu.roll(total, 1, 1), 5, 0)
+        above = pltpu.roll(pltpu.roll(total, self.ny - 1, 1), 3, 0)
+        total = total + jnp.where(self.component, below, above)
         old = held.field[x, :, self.span(z)]
-        keep = held.keep[pl.ds(x * self.pitch + z, 1), :]
-        value = old - (self.component * keep) * (total + ground_spring * old)
-        self.store_node(refs, x, z, value, w_ref)
+        gain = jnp.where(self.component, self.kept_row(refs.gain, x, z), self.kept_row(refs.ahead, x, z))
+        self.store_node(refs, x, z, old - gain * (total + ground_spring * old), w_ref)
 
     def sweep(self, level, layers, split_at, coefficients_at, carried, emit, carry_to):
         for x in layers:
-            vol_ref, dev_ref = coefficients_at(x)
+            tiles_ref, dev_ref = coefficients_at(x)
             z, end = level - 1, self.size_z - level
             side_low = side_high = None
             while z < end:
@@ -220,7 +235,8 @@
                 forces = jnp.dot(self.kmat, rhs, preferred_element_type=jnp.float32)
                 for j in range(cols):
                     here = z + j
-                    vol = vol_ref[pl.ds(x * self.pitch + here, 1), :]
+                    row = self.tile_row(x, here)
+                    vol = tiles_ref[row : row + 1, :]
                     dev = dev_ref[pl.ds(x * self.pitch + here, 1), :]
                     g = []
                     for q in range(4):
@@ -236,7 +252,7 @@
             carried = carry_to
 
 
-Refs = collections.namedtuple("Refs", ("vol", "dev", "keep", "field", "split"))
+Refs = collections.namedtuple("Refs", ("tiles", "dev", "keep", "gain", "ahead", "field", "split"))
 
 
 def gram_tiles(nx, nz, here, w_at, sums):
@@ -259,34 +275,40 @@
     dims,
     load_ref, plastic_ref, modulus_ref, ca_ref, cb_ref, k_ref, scale_ref,
     w0_ref, w1_ref, w2_ref, w3_ref, part_ref, stash_ref,
-    vol_ref, dev_ref, keep_ref, field_ref, split_ref, clow_ref, chigh_ref,
-    sum_ref,
+    tiles_ref, dev_ref, field_ref, split_ref, clow_ref, chigh_ref,
+    sum_ref, keep_ref, gain_ref, ahead_ref,
 ):
-    nx, nz, ny, _, tz, _ = dims
+    nx, nz, ny, tx, tz, _ = dims
     work = Products(dims, k_ref[...], scale_ref)
     pitch = work.pitch
-    refs = Refs(vol_ref, dev_ref, keep_ref, field_ref, split_ref)
+    refs = Refs(tiles_ref, dev_ref, keep_ref, gain_ref, ahead_ref, field_ref, split_ref)
     w_refs = (w0_ref, w1_ref, w2_ref, w3_ref)
     pick(ca_ref, cb_ref, is_odd("curve"), clow_ref, chigh_ref)
+    tiles_ref[...] = jnp.zeros_like(tiles_ref)
+    for tile_x in range(tx):
+        row = (tile_x + 1) * (tz + 2)
+        at = 4 * HALO * nx + tile_x
+        tiles_ref[row : row + 1, :] = clow_ref[at : at + 1, :]
+        tiles_ref[row + 1 : row + 1 + tz, :] = modulus_ref[tile_x * tz : (tile_x + 1) * tz, :]
+        tiles_ref[row + 1 + tz : row + 2 + tz, :] = chigh_ref[at : at + 1, :]
     for own in range(nx):
-        row = (own + HALO) * pitch
-        dev_ref[row + HALO : row + HALO + nz, :] = plastic_ref[own * nz : (own + 1) * nz, :]
-        tile_x = own // TILE
+        x = own + HALO
+        inside = 1.0 - plastic_ref[own * nz : (own + 1) * nz, :]
         for t in range(tz):
-            value = modulus_ref[tile_x * tz + t : tile_x * tz + t + 1, :]
-            first = row + HALO + t * TILE
-            vol_ref[first : first + TILE, :] = jnp.broadcast_to(value, (TILE, ny))
-        at = 4 * HALO * nx + tile_x
-        for ref, first in ((clow_ref, row), (chigh_ref, row + HALO + nz)):
-            vol_ref[first : first + HALO, :] = jnp.broadcast_to(ref[at : at + 1, :], (HALO, ny))
+            row = work.tile_row(x, HALO + t * TILE)
+            first = x * pitch + HALO + t * TILE
+            part = inside[t * TILE : (t + 1) * TILE, :]
+            dev_ref[first : first + TILE, :] = tiles_ref[row : row + 1, :] * part
     for zl in range(HALO):
         at = (3 * HALO + zl) * nx
         for ref, z in ((clow_ref, zl), (chigh_ref, HALO + nz + zl)):
-            dev_ref[pl.ds(HALO * pitch + z, nx, stride=pitch), :] = ref[at : at + nx, :]
+            for tile_x in range(tx):
+                row = work.tile_row(HALO + tile_x * TILE, z)
+                rows = slice(at + tile_x * TILE, at + (tile_x + 1) * TILE)
+                value = tiles_ref[row : row + 1, :] * (1.0 - ref[rows, :])
+                dev_ref[pl.ds((HALO + tile_x * TILE) * pitch + z, TILE, stride=pitch), :] = value
     first, last = HALO + 1, HALO + nx - 1
-    work.mark_kept(refs, range(first, last + 1), lambda x: vol_ref)
-    for own in range(nx):
-        work.deviatoric(refs, own + HALO)
+    work.mark_kept(refs, range(first, last + 1))
     for x in range(first, last + 1):
         own = x - HALO
         for z in range(work.size_z):
@@ -308,11 +330,11 @@
                 work.update_node(refs, refs, x, z, total + before, w_refs[level])
 
         work.sweep(
-            level, layers[:-1], lambda x: split_ref, lambda x: (vol_ref, dev_ref), None, emit, sum_ref
+            level, layers[:-1], lambda x: split_ref, lambda x: (tiles_ref, dev_ref), None, emit, sum_ref
         )
         carried = sum_ref if len(layers) > 1 else None
         work.sweep(
-            level, layers[-1:], lambda x: split_ref, lambda x: (vol_ref, dev_ref), carried, emit, high_ref
+            level, layers[-1:], lambda x: split_ref, lambda x: (tiles_ref, dev_ref), carried, emit, high_ref
         )
     sums = gram_tiles(
         nx, nz, lambda j, x: x in inner_rows(nx, j), lambda j, x: w_refs[j], [None] * len(PAIRS)
@@ -325,39 +347,36 @@
     dims,
     modulus_ref, load_ref, sa_ref, sb_ref, k_ref, scale_ref,
     a0_ref, a1_ref, a2_ref, a3_ref, part_ref, stash_ref,
-    ivol_ref, idev_ref, ikeep_ref, ifield_ref, isplit_ref, clow_ref, chigh_ref,
+    itiles_ref, idev_ref, ifield_ref, isplit_ref, clow_ref, chigh_ref,
     b0_ref, b1_ref, b2_ref, b3_ref, gram_ref,
-    slow_ref, shigh_ref, vol_ref, dev_ref, keep_ref, field_ref, split_ref, sum_ref,
+    slow_ref, shigh_ref, tiles_ref, dev_ref, keep_ref, gain_ref, ahead_ref, field_ref, split_ref, sum_ref,
 ):
-    nx, nz, ny, _, tz, _ = dims
+    nx, nz, ny, tx, tz, _ = dims
     work = Products(dims, k_ref[...], scale_ref)
     pitch, size_x, size_z = work.pitch, work.size_x, work.size_z
-    refs = Refs(vol_ref, dev_ref, keep_ref, field_ref, split_ref)
-    inner = Refs(ivol_ref, idev_ref, ikeep_ref, ifield_ref, isplit_ref)
+    refs = Refs(tiles_ref, dev_ref, keep_ref, gain_ref, ahead_ref, field_ref, split_ref)
+    inner = Refs(tiles_ref, idev_ref, keep_ref, gain_ref, ahead_ref, ifield_ref, isplit_ref)
     a_refs = (a0_ref, a1_ref, a2_ref, a3_ref)
     b_refs = (b0_ref, b1_ref, b2_ref, b3_ref)
     pick(sa_ref, sb_ref, is_odd("sub"), slow_ref, shigh_ref)
     own_layers = range(HALO, HALO + nx)
+    tiles_ref[...] = itiles_ref[...]
+    at = 4 * HALO * size_z
+    for side_ref, row in ((slow_ref, 0), (shigh_ref, (tx + 1) * (tz + 2))):
+        tiles_ref[row : row + tz + 2, :] = side_ref[at : at + tz + 2, :]
     for x in range(size_x - 1):
         if x in own_layers:
             continue
-        row = x * pitch
         side_ref, xl = (slow_ref, x) if x < HALO else (shigh_ref, x - HALO - nx)
-        at = (3 * HALO + xl) * size_z
-        dev_ref[row : row + size_z, :] = side_ref[at : at + size_z, :]
-        at = 4 * HALO * size_z
-        for t in range(tz):
-            first = row + HALO + t * TILE
-            value = side_ref[at + 1 + t : at + 2 + t, :]
-            vol_ref[first : first + TILE, :] = jnp.broadcast_to(value, (TILE, ny))
-        for rim, first in ((at, row), (at + 1 + tz, row + HALO + nz)):
-            vol_ref[first : first + HALO, :] = jnp.broadcast_to(side_ref[rim : rim + 1, :], (HALO, ny))
+        inside = 1.0 - side_ref[(3 * HALO + xl) * size_z : (3 * HALO + xl + 1) * size_z, :]
+        bounds = [0, *range(HALO, HALO + nz + 1, TILE), size_z]
+        for first, last in zip(bounds, bounds[1:]):
+            row = work.tile_row(x, first)
+            value = tiles_ref[row : row + 1, :] * inside[first:last, :]
+            dev_ref[x * pitch + first : x * pitch + last, :] = value
     started = range(HALO + 1, HALO + nx)
     rest = [x for x in range(size_x) if x not in started]
-    work.mark_kept(refs, rest, lambda x: ivol_ref if x in own_layers else vol_ref)
-    for x in range(size_x - 1):
-        if x not in own_layers:
-            work.deviatoric(refs, x)
+    work.mark_kept(refs, range(size_x))
     for x in rest:
         for z in range(size_z):
             if x < HALO:
@@ -373,15 +392,12 @@
             work.start_node(refs, x, z, rows, b0_ref)
 
     held = {x: inner if x in started else refs for x in range(size_x)}
-    keeps = dict(held)
 
     def update(x, z, total, level):
-        source = keeps[x]._replace(field=held[x].field)
-        work.update_node(refs, source, x, z, total, b_refs[level])
+        work.update_node(refs, held[x], x, z, total, b_refs[level])
 
     def coefficients_at(x):
-        source = inner if x in own_layers else refs
-        return source.vol, source.dev
+        return tiles_ref, (inner if x in own_layers else refs).dev
 
     for level in range(1, ITERS + 1):
         done = []
@@ -555,33 +571,36 @@
     sub_a = exchange(sub_a, "sub", 0)
     basis_shape = (kept((3 * nx * nz, ny), f32),) * (ITERS + 1)
     coefficient = (size_x * pitch, ny)
+    tile_rows = (round_up((tx + 2) * (tz + 2), 8), ny)
+    class_rows = (round_up((2 * tx + 3) * (2 * tz + 3), 8), ny)
     field = (size_x, 8, size_z * ny)
     split = (size_x, 16, size_z * ny)
     stash = (2 * ITERS, 8, size_z * ny)
 
     def solve(scale):
-        *first, part, stashed, vol, dev, keep, fields, splits, low, high = pl.pallas_call(
+        *first, part, stashed, tiles, dev, fields, splits, low, high = pl.pallas_call(
             functools.partial(inner_product_kernel, dims),
             out_shape=basis_shape + (
                 kept((8 * len(PAIRS), ny), f32), kept(stash, f32),
-                kept(coefficient, f32), kept(coefficient, f32), kept(coefficient, f32),
+                kept(tile_rows, f32), kept(coefficient, f32),
                 kept(field, f32), kept(split, jnp.bfloat16),
                 kept((curve_rows, ny), f32), kept((curve_rows, ny), f32),
             ),
             in_specs=[vmem] * 7,
-            out_specs=(vmem,) * (ITERS + 10),
-            scratch_shapes=[pltpu.VMEM((8, size_z * ny), f32)],
+            out_specs=(vmem,) * (ITERS + 9),
+            scratch_shapes=[pltpu.VMEM((8, size_z * ny), f32)] + [pltpu.VMEM(class_rows, f32)] * 3,
             compiler_params=grant,
             name="inner_products",
         )(*near(load, plastic, modulus, curve_a, curve_b, k_both, scale))
         *second, gram = pl.pallas_call(
             functools.partial(outer_product_kernel, dims),
             out_shape=basis_shape + (kept((count, 1, ny), f32),),
-            in_specs=[vmem] * (ITERS + 16),
+            in_specs=[vmem] * (ITERS + 15),
             out_specs=(vmem,) * (ITERS + 2),
             scratch_shapes=[
                 pltpu.VMEM((sub_rows, ny), f32), pltpu.VMEM((sub_rows, ny), f32),
-                pltpu.VMEM(coefficient, f32), pltpu.VMEM(coefficient, f32), pltpu.VMEM(coefficient, f32),
+                pltpu.VMEM(tile_rows, f32), pltpu.VMEM(coefficient, f32),
+                pltpu.VMEM(class_rows, f32), pltpu.VMEM(class_rows, f32), pltpu.VMEM(class_rows, f32),
                 pltpu.VMEM(field, f32), pltpu.VMEM(split, jnp.bfloat16),
                 pltpu.VMEM((8, size_z * ny), f32),
             ],
@@ -589,7 +608,7 @@
             name="outer_products",
         )(*near(
             modulus, load, sub_a, sub_b, k_both, scale,
-            *first, part, stashed, vol, dev, keep, fields, splits, low, high,
+            *first, part, stashed, tiles, dev, fields, splits, low, high,
         ))
         gram = lax.all_to_all(gram, AXES, 0, 0)
         return pl.pallas_call(

time: 33.2 us -> 32.5 us (0.979)
  Pallas kernels: 7.54 us -> 6.21 us
  blocking collectives: 19.9 us -> 20.5 us
    pallas_call x1, Pallas kernels: 2.55 us -> 1.8 us  [solve(): pl.pallas_call(functools.partial(outer_product_kernel, dims), out_shape=b...]
    all_to_all x1, blocking collectives: 19.9 us -> 20.5 us  [solve(): gram = lax.all_to_all(gram, AXES, 0, 0)]
    pallas_call x1, Pallas kernels: 1.96 us -> 1.39 us  [solve(): pl.pallas_call(functools.partial(inner_product_kernel, dims), out_shape=b...]
  transfers between devices with their start and end apart: 4 -> 4, of which waited for: 1 -> 1; matrix products, arithmetic and copies ran while one was open for 0% -> 0% of each run, Pallas kernels for 9% -> 8%
where the time goes in v6:
time: 32.5 us; the launch traced here: 32.2 us
  blocking collectives  20.5 us (63%)
  Pallas kernels  6.21 us (19%)
  starting transfers between devices  4.42 us (14%)
  between operations  0.75 us (2%)
  waiting for transfers between devices  0.39 us (1%)
    all_to_all x1, blocking collectives, solve(): gram = lax.all_to_all(gram, AXES, 0, 0)  20.5 us
    ppermute x4, starting transfers between devices, exchange(): return lax.ppermute(value, axis, pairs)  4.42 us
    pallas_call x1, Pallas kernels, solve(): pl.pallas_call(functools.partial(outer_product_kernel, dims), out_shape=b...  1.8 us
    pallas_call x1, Pallas kernels, solve(): pl.pallas_call(functools.partial(inner_product_kernel, dims), out_shape=b...  1.39 us
    pallas_call x1, Pallas kernels, local(): pl.pallas_call(setup_kernel, out_shape=(kept((64, 128), jnp.bfloat16), ke...  1.05 us
    pallas_call x1, Pallas kernels, local(): pl.pallas_call(functools.partial(curve_message_kernel, dims), out_shape=(...  1.03 us
    pallas_call x1, Pallas kernels, solve(): pl.pallas_call(functools.partial(finish_kernel, dims), out_shape=(shape((...  0.89 us
  transfers between devices with their start and end apart: 4, of which 1 were waited for; matrix products, arithmetic and copies ran while one was open for 0% of the time, Pallas kernels for 8%

profile of v6, /device:TPU:0, one launch (start us, length us, event | category | flops | bytes accessed | tf_op | source)
XLA Modules:
  0.0 32.2 jit_solution(12715742176866686789)
XLA Ops:
  0.6 0.0 copy-start
  0.6 0.0 copy-start.2
  0.7 0.0 copy-start.3
  0.7 1.0 %curve_message.1 = (f32[104,128]{1,0:T(8,128)S(1)}, f32[104,128]{1,0:T(8,128)S(1)}, f32[8,128]{1,0:T(8,128)S(1)}) custom-call(s32[1,1,16]{2,1,0:T(1,128)} %tile_ref.1, f32[4]{0:T(128)} %moduli_ref.3, f32[192,128]{1,0:T(8,128)} %bitcast.7, f32[64,128]{1,0:T(8,128)} %bitcast.12), custom_call_target="tpu_custom_call" | custom-call | tf_op jit(solution)/shard_map/curve_message/pallas_call | solution.py:543
  1.7 0.0 copy-start.1
  1.7 3.0 %collective-permute-start = (f32[104,128]{1,0:T(8,128)S(1)}, f32[104,128]{1,0:T(8,128)S(1)}, u32[]{:S(2)}, u32[]{:S(2)}) collective-permute-start(f32[104,128]{1,0:T(8,128)S(1)} %get-tuple-element.87), channel_id=1, source_target_pairs={{0,4},{4,0},{8,12},{12,8},{16,20},{20,16},{24,28},{28,24},{1,5},{5... | collective-permute-start | bytes 159752 | tf_op jit(solution)/shard_map/ppermute | solution.py:33
  4.7 0.7 %collective-permute-start.1 = (f32[104,128]{1,0:T(8,128)S(1)}, f32[104,128]{1,0:T(8,128)S(1)}, u32[]{:S(2)}, u32[]{:S(2)}) collective-permute-start(f32[104,128]{1,0:T(8,128)S(1)} %get-tuple-element.88), channel_id=1, source_target_pairs={{4,8},{8,4},{12,16},{16,12},{20,24},{24,20},{5,9},{9,5},{13,17},{1... | collective-permute-start | bytes 159752 | tf_op jit(solution)/shard_map/ppermute | solution.py:33
  5.4 0.0 copy-done.2
  5.4 0.0 copy-done.3
  5.4 1.0 %setup.1 = (bf16[64,128]{1,0:T(8,128)(2,1)S(1)}, f32[8,128]{1,0:T(8,128)S(1)}) custom-call(f32[4]{0:T(128)} %moduli_ref.3, f32[24,24]{1,0:T(8,128)S(1)} %copy-done.2, f32[24,24]{1,0:T(8,128)S(1)} %copy-done.3, f32[8,128]{1,0:T(8,128)S(1)} %get-tuple-element.86._.modulus_ref), custom_call_target="tpu_custom_call" | custom-call | tf_op jit(solution)/shard_map/setup/pallas_call | solution.py:551
  6.5 0.4 %collective-permute-done.ra_ref.ca_ref = f32[104,128]{1,0:T(8,128)S(1)} collective-permute-done((f32[104,128]{1,0:T(8,128)S(1)}, f32[104,128]{1,0:T(8,128)S(1)}, u32[]{:S(2)}, u32[]{:S(2)}) %collective-permute-start) | collective-permute-done | bytes 53280 | tf_op jit(solution)/shard_map/ppermute | solution.py:33
  6.9 0.0 collective-permute-done.1.rb_ref.cb_ref
  6.9 0.0 copy-done
  6.9 0.0 copy-done.1
  6.9 0.1 sub_message.1
  6.9 0.1 collective-permute-start.2
  7.0 0.7 %collective-permute-start.3 = (f32[176,128]{1,0:T(8,128)S(1)}, f32[176,128]{1,0:T(8,128)S(1)}, u32[]{:S(2)}, u32[]{:S(2)}) collective-permute-start(f32[176,128]{1,0:T(8,128)S(1)} %get-tuple-element.91), channel_id=1, source_target_pairs={{1,2},{2,1},{5,6},{6,5},{9,10},{10,9},{13,14},{14,13},{17,18},{18,... | collective-permute-start | bytes 270344 | tf_op jit(solution)/shard_map/ppermute | solution.py:33
  7.7 1.4 %inner_products.3 = (f32[192,128]{1,0:T(8,128)S(1)}, f32[192,128]{1,0:T(8,128)S(1)}, f32[192,128]{1,0:T(8,128)S(1)}, f32[192,128]{1,0:T(8,128)S(1)}, f32[80,128]...) custom-call(f32[192,128]{1,0:T(8,128)S(1)} %bitcast.9, ...), custom_call_target="tpu_custom_call" | custom-call | tf_op jit(solution)/shard_map/inner_products/pallas_call | solution.py:581
  9.1 0.0 collective-permute-done.2.sa_ref
  9.1 0.0 collective-permute-done.3.sb_ref
  9.1 1.8 %outer_products.3 = (f32[192,128]{1,0:T(8,128)S(1)}, f32[192,128]{1,0:T(8,128)S(1)}, f32[192,128]{1,0:T(8,128)S(1)}, f32[192,128]{1,0:T(8,128)S(1)}, f32[32,1,128]{2,1,0:T(1,128)S(1)}) custom-call(f32[8,128]{1,0:T(8,128)S(1)} %get-tuple-element.86._.modulus_ref, f32[192,128]{1,0:T(8,128)S(1)} %bitcast.10, f32[176,128]{1,0:T(8,128)S(1)} %collective-permute-done.2.sa_ref, ...), custom_call_target="tpu_custom_call" | custom-call | tf_op jit(solution)/shard_map/outer_products/pallas_call | solution.py:595
  10.9 20.5 %all_to_all.10.gram_ref = f32[32,1,128]{2,1,0:T(1,128)S(1)} all-to-all(f32[32,1,128]{2,1,0:T(1,128)S(1)} %get-tuple-element.105), channel_id=1, replica_groups=mesh['curve'=8,'sub'=4] {'curve','sub'}, dimensions={0} | all-to-all | bytes 32768 | tf_op jit(solution)/shard_map/all_to_all | solution.py:613
  31.4 0.9 %finish.3 = (f32[192,128]{1,0:T(8,128)}, f32[192,128]{1,0:T(8,128)}, f32[8,128]{1,0:T(8,128)S(1)}, s32[1,1]{1,0:T(1,128)S(4)}) custom-call(f32[32,1,128]{2,1,0:T(1,128)S(1)} %all_to_all.10.gram_ref, f32[8,128]{1,0:T(8,128)S(1)} %get-tuple-element.89._.scale_ref, f32[192,128]{1,0:T(8,128)S(1)} %get-tuple-element.93.a0_ref.refs_0_, ...), custom_call_target="tpu_custom_call" | custom-call | tf_op jit(solution)/shard_map/finish/pallas_call | solution.py:614
  (1 shorter events, 0.0 us)
Async XLA Ops:
  0.6 6.2 %copy-start = (f32[3,8,8,128]{3,2,1,0:T(8,128)S(1)}, f32[3,8,8,128]{3,2,1,0:T(8,128)}, u32[]{:S(2)}) copy-start(f32[3,8,8,128]{3,2,1,0:T(8,128)} %param.8) | copy-start | bytes 294916
  0.6 4.8 %copy-start.2 = (f32[24,24]{1,0:T(8,128)S(1)}, f32[24,24]{1,0:T(8,128)}, u32[]{:S(2)}) copy-start(f32[24,24]{1,0:T(8,128)} %kv_ref.1) | copy-start | bytes 6916
  0.7 4.8 %copy-start.3 = (f32[24,24]{1,0:T(8,128)S(1)}, f32[24,24]{1,0:T(8,128)}, u32[]{:S(2)}) copy-start(f32[24,24]{1,0:T(8,128)} %kd_ref.1) | copy-start | bytes 6916
  1.7 5.2 %copy-start.1 = (f32[8,8,128]{2,1,0:T(8,128)S(1)}, f32[8,8,128]{2,1,0:T(8,128)}, u32[]{:S(2)}) copy-start(f32[8,8,128]{2,1,0:T(8,128)} %param.9) | copy-start | bytes 98308
  1.7 5.1 %collective-permute-start = (f32[104,128]{1,0:T(8,128)S(1)}, f32[104,128]{1,0:T(8,128)S(1)}, u32[]{:S(2)}, u32[]{:S(2)}) collective-permute-start(f32[104,128]{1,0:T(8,128)S(1)} %get-tuple-element.87), channel_id=1, source_target_pairs={{0,4},{4,0},{8,12},{12,8},{16,20},{20,16},{24,28},{28,24},{1,5},{5... | collective-permute-start | bytes 159752 | tf_op jit(solution)/shard_map/ppermute | solution.py:33
  4.7 2.1 %collective-permute-start.1 = (f32[104,128]{1,0:T(8,128)S(1)}, f32[104,128]{1,0:T(8,128)S(1)}, u32[]{:S(2)}, u32[]{:S(2)}) collective-permute-start(f32[104,128]{1,0:T(8,128)S(1)} %get-tuple-element.88), channel_id=1, source_target_pairs={{4,8},{8,4},{12,16},{16,12},{20,24},{24,20},{5,9},{9,5},{13,17},{1... | collective-permute-start | bytes 159752 | tf_op jit(solution)/shard_map/ppermute | solution.py:33
  6.9 2.1 %collective-permute-start.2 = (f32[176,128]{1,0:T(8,128)S(1)}, f32[176,128]{1,0:T(8,128)S(1)}, u32[]{:S(2)}, u32[]{:S(2)}) collective-permute-start(f32[176,128]{1,0:T(8,128)S(1)} %get-tuple-element.90), channel_id=1, source_target_pairs={{0,1},{1,0},{2,3},{3,2},{4,5},{5,4},{6,7},{7,6},{8,9},{9,8},{10,11... | collective-permute-start | bytes 270344 | tf_op jit(solution)/shard_map/ppermute | solution.py:33
  7.0 2.1 %collective-permute-start.3 = (f32[176,128]{1,0:T(8,128)S(1)}, f32[176,128]{1,0:T(8,128)S(1)}, u32[]{:S(2)}, u32[]{:S(2)}) collective-permute-start(f32[176,128]{1,0:T(8,128)S(1)} %get-tuple-element.91), channel_id=1, source_target_pairs={{1,2},{2,1},{5,6},{6,5},{9,10},{10,9},{13,14},{14,13},{17,18},{18,... | collective-permute-start | bytes 270344 | tf_op jit(solution)/shard_map/ppermute | solution.py:33
